TPU v7x, 128 devices: a whole 4x4x4 slice. The times are simulated.
128 devices in a mesh: mer: 16 (over x, z), box: 8 (over y, core).
Axes of the slice: x: 4, y: 4, z: 4, core: 2. Of those that a mesh axis runs over, the one named last changes fastest.
Arguments:
- annulus: float32 [25, 512, 2048], P(None, 'box', 'mer'), may hold values from -6 to 6
- annulus_prev: float32 [25, 512, 2048], P(None, 'box', 'mer'), may hold values from -6 to 6
- derivative: float32 [25, 25], replicated, may hold values from -1.25 to 1.25
- radial_modulus: float32 [25, 2048], P(None, 'mer'), may hold values from 0.5 to 2
- shear_modulus: float32 [25, 2048], P(None, 'mer'), may hold values from 0.5 to 2
- node_mass: float32 [25, 2048], P(None, 'mer'), may hold values from 1 to 4
- element_modes: int32 [2048], P('mer'), may hold values from 1 to 256
- upper_rows: int32 [4096], P('mer'), may hold values from 0 to 3199
- lower_rows: int32 [4096], P('mer'), may hold values from 0 to 3199
- coupling_rows: int32 [32768], P('mer'), may hold values from 0 to 3199
- coupling_target: int32 [32768, 1], P('mer'), may hold values from 0 to 127; in each aligned block of 2048 rows (0 to 2047, 2048 to 4095, ...) at most 32 rows name the same one
- box_field: float32 [131072], P(('mer', 'box')), may hold values from -6 to 6
- box_prev: float32 [131072], P(('mer', 'box')), may hold values from -6 to 6
- box_angle: float32 [131072], P(('mer', 'box')), may hold values from -3.140625 to 3.140625
- box_spring: float32 [131072], P(('mer', 'box')), may hold values from 0.5 to 2
- box_mass: float32 [131072], P(('mer', 'box')), may hold values from 1 to 4
- box_weight: float32 [131072], P(('mer', 'box')), may hold values from 0.05 to 0.5
- box_slot: int32 [131072], P(('mer', 'box')), may hold values from 0 to 511, as said below
Outputs:
- annulus_out: float32 [25, 512, 2048], P(None, 'box', 'mer')
- box_out: float32 [131072], P(('mer', 'box'))
Inputs may be any that keep to these rules, and one draw needn't show every extreme that they name: `lower_rows`: part rows, paired with the previous part's upper rows. `coupling_target`: among the 2048 rows of one part no box part is named more than 32 times, and some box part exactly 32 times. `box_slot`: slot p * 16 + i of the node's box part: the p-th coupling row that part i sends there; slots that no row fills hold zeros. Among the 1024 nodes of one box part, exactly 64 read slots of each meridional part i.
All inputs are finite; a program needn't handle non-finite values.
Results may differ from a plain program's by a relative error of at most 0.0003.
Values sent between devices are 32-bit elements; how exact they have to be, the bound alone decides.
A program may use at most 128 MiB of HBM per device.

v0:
```python
import functools

import jax
import jax.numpy as jnp
from jax import lax
from jax.experimental import pallas as pl
from jax.experimental.pallas import tpu as pltpu
from jax.sharding import PartitionSpec as P

F32 = jnp.float32
BF16 = jnp.bfloat16
I32 = jnp.int32
MESH = pl.DeviceIdType.MESH

MER, BOX = 16, 8
MODES = 256
NODES, COLS, ELEMS = 25, 64, 128
PAIRS = 13
GROUPS = 32
ALL_GROUPS = 36
ROWS = 64
STEP_SCALE = 0.25


def iota(shape, dim):
    return lax.broadcasted_iota(I32, shape, dim)


def hot(mask):
    return jnp.where(mask, 1.0, 0.0).astype(BF16)


def dot(a, b):
    return jnp.dot(a, b, preferred_element_type=F32)


def dot_nt(a, b):
    return lax.dot_general(a, b, (((1,), (1,)), ((), ())), preferred_element_type=F32)


def split2(x):
    hi = x.astype(BF16)
    return hi, (x - hi.astype(F32)).astype(BF16)


def split3(x):
    hi = x.astype(BF16)
    rest = x - hi.astype(F32)
    mid = rest.astype(BF16)
    return hi, mid, (rest - mid.astype(F32)).astype(BF16)


def take_lanes(x, index):
    return jnp.take_along_axis(x, index, axis=1, mode="promise_in_bounds")


def sincos(x):
    k = jnp.floor(x * 0.6366197723675814 + 0.5)
    r = x - k * 1.5703125
    r = r - k * 4.837512969970703125e-4
    r = r - k * 7.54978995489188216e-8
    z = r * r
    s = ((-1.9515295891e-4 * z + 8.3321608736e-3) * z - 1.6666654611e-1) * z * r + r
    c = ((2.443315711809948e-5 * z - 1.388731625493765e-3) * z + 4.166664568298827e-2) * z * z
    c = c - 0.5 * z + 1.0
    q = k.astype(I32)
    odd = (q & 1) == 1
    sine = jnp.where(odd, c, s)
    cosine = jnp.where(odd, s, c)
    sine = jnp.where((q & 2) == 2, -sine, sine)
    cosine = jnp.where(((q + 1) & 2) == 2, -cosine, cosine)
    return sine, cosine


def setup_kernel(
    slot_ref, angle_ref, spring_ref, mass_ref, weight_ref, now_ref, before_ref,
    rows_ref, target_ref, lower_ref, upper_ref,
    send_ref, dest_ref, node_ref, elem_ref, fields,
):
    tri = hot(iota((128, 128), 0) < iota((128, 128), 1))
    slot = slot_ref[...]
    part = slot & (MER - 1)
    sources = [
        angle_ref[...], (slot >> 4).astype(F32), spring_ref[...], mass_ref[...],
        weight_ref[...], now_ref[...], before_ref[...], jnp.zeros((8, 128), F32),
    ]
    for r in range(8):
        for f in range(8):
            fields[r, f : f + 1, :] = sources[f][r : r + 1, :]
    base = jnp.zeros((MER, 1), F32)
    total = jnp.zeros((24, 1024), F32)
    for r in range(8):
        mine = part[r : r + 1, :]
        member = jnp.where(iota((MER, 128), 0) == mine, 1.0, 0.0)
        rank = dot(member.astype(BF16), tri) + base
        place = jnp.sum(member * rank, axis=0, keepdims=True).astype(I32)
        base = base + jnp.sum(member, axis=1, keepdims=True)
        dest = mine * 64 + place
        dest_ref[r : r + 1, :] = dest
        order = hot(iota((1024, 128), 0) == dest)
        pieces = jnp.concatenate(split3(fields[r]), axis=0)
        total = total + dot_nt(pieces, order)
    sorted_fields = total[0:8] + (total[8:16] + total[16:24])
    for m in range(8):
        send_ref[m] = sorted_fields[:, m * 128 : (m + 1) * 128]

    rows = rows_ref[...]
    target = target_ref[...]
    reader = (target & (BOX - 1)) * MER + (target >> 3)
    node1 = ((rows >> 7) + 1).astype(F32)
    elem = (rows & 127).astype(F32)
    count = jnp.zeros((128, 1), F32)
    table = jnp.zeros((64, 128), F32)
    for r in range(16):
        mine = reader[r : r + 1, :]
        member = jnp.where(iota((128, 128), 0) == mine, 1.0, 0.0)
        rank = dot(member.astype(BF16), tri) + count
        place = jnp.sum(member * rank, axis=0, keepdims=True).astype(I32)
        count = count + jnp.sum(member, axis=1, keepdims=True)
        lane = (mine & 3) * 32 + place
        group = iota((GROUPS, 128), 0) == (mine >> 2)
        values = jnp.concatenate(
            [
                jnp.where(group, jnp.broadcast_to(node1[r : r + 1, :], (GROUPS, 128)), 0.0),
                jnp.where(group, jnp.broadcast_to(elem[r : r + 1, :], (GROUPS, 128)), 0.0),
            ],
            axis=0,
        ).astype(BF16)
        table = table + dot_nt(values, hot(iota((128, 128), 0) == lane))
    node_ref[0:GROUPS, :] = table[0:GROUPS].astype(I32) - 1
    elem_ref[0:GROUPS, :] = table[GROUPS : 2 * GROUPS].astype(I32)
    for k, ref in enumerate((lower_ref, upper_ref)):
        edge = ref[...]
        node_ref[GROUPS + 2 * k : GROUPS + 2 * k + 2, :] = edge >> 7
        elem_ref[GROUPS + 2 * k : GROUPS + 2 * k + 2, :] = edge & 127


def halves(even, odd, half):
    low = jnp.where(half == 0, even, pltpu.roll(even, 64, 1))
    high = jnp.where(half == 1, odd, pltpu.roll(odd, 64, 1))
    return jnp.where(iota((8, 128), 1) < 64, low, high)


def greet(partners):
    barrier = pltpu.get_barrier_semaphore()
    for device in partners:
        pl.semaphore_signal(barrier, inc=1, device_id=device, device_id_type=MESH)
    pl.semaphore_wait(barrier, len(partners))


def distribute_kernel(
    send_ref, own_ref, angle_ref, place_ref, received, share, shared,
    send_sem, recv_sem, share_send, share_recv,
):
    i = lax.axis_index("mer")
    j = lax.axis_index("box")
    mer_peers = [lax.rem(i + o, MER) for o in range(1, MER)]
    box_peers = [lax.rem(j + o, BOX) for o in range(1, BOX)]
    greet([(q, j) for q in mer_peers] + [(i, q) for q in box_peers])
    copies = []
    for o, q in enumerate(mer_peers):
        copy = pltpu.make_async_remote_copy(
            src_ref=send_ref.at[q // 2],
            dst_ref=received.at[i],
            send_sem=send_sem.at[o],
            recv_sem=recv_sem.at[o],
            device_id=(q, j),
            device_id_type=MESH,
        )
        copy.start()
        copies.append(copy)
    received[i] = send_ref[i // 2]
    for copy in copies:
        copy.wait()
    half = lax.rem(i, 2)
    fields = []
    for f in range(7):
        even = jnp.concatenate([received[2 * r, f : f + 1, :] for r in range(8)], axis=0)
        odd = jnp.concatenate([received[2 * r + 1, f : f + 1, :] for r in range(8)], axis=0)
        fields.append(halves(even, odd, half))
    share[0] = fields[0]
    share[1] = fields[1]
    copies = []
    for o, q in enumerate(box_peers):
        copy = pltpu.make_async_remote_copy(
            src_ref=share,
            dst_ref=shared.at[j],
            send_sem=share_send.at[o],
            recv_sem=share_recv.at[o],
            device_id=(i, q),
            device_id_type=MESH,
        )
        copy.start()
        copies.append(copy)
    for f in range(5):
        own_ref[f] = fields[f + 2]
    shared[j] = share[...]
    for copy in copies:
        copy.wait()
    for b in range(BOX):
        angle_ref[b * 8 : (b + 1) * 8, :] = shared[b, 0]
        place_ref[b * 8 : (b + 1) * 8, :] = shared[b, 1].astype(I32)


def harmonics(j, angle_ref, harmonic_ref):
    sub = iota((8, 128), 0).astype(F32)
    first = (lax.rem(j, 4) * 64).astype(F32)
    is_sine = j >= 4

    def body(row, carry):
        angle = jnp.broadcast_to(angle_ref[pl.ds(row, 1), :], (8, 128))
        base_sin, base_cos = sincos(angle * (sub + first))
        step_sin, step_cos = sincos(angle * (sub * 8.0))
        a = jnp.where(is_sine, base_sin, base_cos)
        b = jnp.where(is_sine, -base_cos, base_sin)
        for t in range(8):
            harmonic_ref[row, t * 8 : (t + 1) * 8, :] = (
                a * step_cos[t : t + 1, :] - b * step_sin[t : t + 1, :]
            )
        return carry

    lax.fori_loop(0, ROWS, body, 0)


def gather_rows(values_ref, node, elem, groups):
    index = jnp.broadcast_to(elem, (8, 128))
    node = jnp.broadcast_to(node, (8, 128))
    acc = [jnp.zeros((8, 128), F32) for _ in range(8)]
    for a in range(NODES):
        mask = node == a
        for c in range(8):
            taken = take_lanes(values_ref[a * 64 + c * 8 : a * 64 + c * 8 + 8, :], index)
            acc[c] = jnp.where(mask, taken, acc[c])
    return acc


def fill_table(values_ref, node_ref, elem_ref, table_ref):
    def body(g, carry):
        acc = gather_rows(values_ref, node_ref[pl.ds(g, 1), :], elem_ref[pl.ds(g, 1), :], 1)
        for c in range(8):
            table_ref[g, c * 8 : (c + 1) * 8, :] = acc[c]
        return carry

    lax.fori_loop(0, GROUPS, body, 0)


def node_lane(place, odd):
    return place + (iota((1, 128), 1) >> 6) * 32 + odd * 64


def sample_nodes(table_ref, place_ref, harmonic_ref, partial_ref):
    def body(g, carry):
        for odd in range(2):
            row = 2 * g + odd
            index = jnp.broadcast_to(node_lane(place_ref[pl.ds(row, 1), :], odd), (8, 128))
            acc = jnp.zeros((8, 128), F32)
            for c in range(8):
                taken = take_lanes(table_ref[g, c * 8 : (c + 1) * 8, :], index)
                acc = acc + taken * harmonic_ref[row, c * 8 : (c + 1) * 8, :]
            partial_ref[pl.ds(row, 1), :] = jnp.sum(acc, axis=0, keepdims=True)
        return carry

    lax.fori_loop(0, GROUPS, body, 0)


def compute_force(j, values_ref, deriv_ref, deriv_t_ref, radial_ref, shear_ref, force_ref):
    deriv = deriv_ref[...]
    deriv_t = deriv_t_ref[...]
    radial = radial_ref[...]
    shear = shear_ref[...]
    first = lax.rem(j, 4) * 64

    def body(k, carry):
        x = jnp.concatenate(
            [values_ref[pl.ds(k * 8 + c, NODES, stride=64), :] for c in range(8)], axis=1
        )
        gradient = jnp.dot(deriv, x, precision=lax.Precision.HIGHEST, preferred_element_type=F32)
        flux = gradient * jnp.concatenate([radial] * 8, axis=1)
        back = jnp.dot(deriv_t, flux, precision=lax.Precision.HIGHEST, preferred_element_type=F32)
        for c in range(8):
            wave = (first + k * 8 + c).astype(F32) * (2.0 / MODES)
            lanes = slice(c * 128, (c + 1) * 128)
            force_ref[pl.ds(k * 8 + c, NODES, stride=64), :] = (
                -back[:, lanes] - shear * (wave * wave) * x[:, lanes]
            )
        return carry

    lax.fori_loop(0, 8, body, 0)


def edge_forces(force_ref, node_ref, elem_ref, edge_ref):
    def body(g, carry):
        acc = gather_rows(
            force_ref, node_ref[pl.ds(GROUPS + g, 1), :], elem_ref[pl.ds(GROUPS + g, 1), :], 1
        )
        for c in range(8):
            edge_ref[g, c * 8 : (c + 1) * 8, :] = acc[c]
        return carry

    lax.fori_loop(0, 4, body, 0)


def front(j, values_ref, node_ref, elem_ref, place_ref, harmonic_ref, table_ref,
          deriv_ref, deriv_t_ref, radial_ref, shear_ref, partial_ref, force_ref, edge_ref):
    fill_table(values_ref, node_ref, elem_ref, table_ref)
    sample_nodes(table_ref, place_ref, harmonic_ref, partial_ref)
    compute_force(j, values_ref, deriv_ref, deriv_t_ref, radial_ref, shear_ref, force_ref)
    edge_forces(force_ref, node_ref, elem_ref, edge_ref)


def slot_reactions(drive_ref, harmonic_ref, place_ref, edge_ref, high_ref, low_ref):
    def body(g, carry):
        pieces, hots = [], []
        for odd in range(2):
            row = 2 * g + odd
            x = harmonic_ref[row] * drive_ref[pl.ds(row, 1), :]
            pieces.append(split2(x))
            lane = node_lane(place_ref[pl.ds(row, 1), :], odd)
            hots.append(hot(iota((128, 128), 0) == lane))
        left = jnp.concatenate([pieces[0][0], pieces[1][0], pieces[0][1], pieces[1][1]], axis=1)
        right = jnp.concatenate(hots + hots, axis=1)
        high, low = split2(dot_nt(left, right))
        high_ref[g] = high
        low_ref[g] = low
        return carry

    lax.fori_loop(0, GROUPS, body, 0)
    for g in range(4):
        high, low = split2(edge_ref[g])
        high_ref[GROUPS + g] = high
        low_ref[GROUPS + g] = low


def scatter_slots(node_ref, elem_ref, high_ref, low_ref, left_ref, sum_ref):
    sum_ref[...] = jnp.zeros_like(sum_ref)

    def body(t, carry):
        hots = []
        for h in range(2):
            g = 2 * t + h
            node = node_ref[pl.ds(g, 1), :]
            lane = (node & 1) * 128 + elem_ref[pl.ds(g, 1), :]
            hots.append(hot(iota((256, 128), 0) == lane))
            pair = node >> 1
            high = high_ref[g]
            low = low_ref[g]
            for a in range(PAIRS):
                mask = jnp.broadcast_to(hot(pair == a), (COLS, 128))
                left_ref[a * 64 : (a + 1) * 64, h * 128 : (h + 1) * 128] = high * mask
                left_ref[a * 64 : (a + 1) * 64, 256 + h * 128 : 384 + h * 128] = low * mask
        right = jnp.concatenate(hots + hots, axis=1)
        sum_ref[...] += dot_nt(left_ref[...], right)
        return carry

    lax.fori_loop(0, ALL_GROUPS // 2, body, 0)


def advance(j, now_ref, before_ref, force_ref, sum_ref, mass_ref, modes_ref, next_ref):
    order = lax.rem(j, 4) * 64 + iota((COLS, 128), 0)
    live = jnp.where(order < modes_ref[...], STEP_SCALE, 0.0)
    for a in range(NODES):
        rows = slice(a * 64, (a + 1) * 64)
        pair = a // 2
        lanes = slice((a % 2) * 128, (a % 2) * 128 + 128)
        total = force_ref[rows, :] + sum_ref[pair * 64 : (pair + 1) * 64, lanes]
        next_ref[rows, :] = (
            2.0 * now_ref[rows, :] - before_ref[rows, :] + live * total / mass_ref[a : a + 1, :]
        )


def first_kernel(
    angle_ref, place_ref, now_ref, node_ref, elem_ref, deriv_ref, deriv_t_ref, radial_ref,
    shear_ref, harmonic_ref, partial_ref, force_ref, edge_ref, table_ref,
):
    j = lax.axis_index("box")
    harmonics(j, angle_ref, harmonic_ref)
    front(j, now_ref, node_ref, elem_ref, place_ref, harmonic_ref, table_ref, deriv_ref,
          deriv_t_ref, radial_ref, shear_ref, partial_ref, force_ref, edge_ref)


def middle_kernel(
    drive_ref, edge_in_ref, harmonic_ref, place_ref, now_ref, before_ref, force_in_ref,
    node_ref, elem_ref, deriv_ref, deriv_t_ref, radial_ref, shear_ref, mass_ref, modes_ref,
    next_ref, partial_ref, force_ref, edge_ref,
    table_ref, high_ref, low_ref, left_ref, sum_ref,
):
    j = lax.axis_index("box")
    slot_reactions(drive_ref, harmonic_ref, place_ref, edge_in_ref, high_ref, low_ref)
    scatter_slots(node_ref, elem_ref, high_ref, low_ref, left_ref, sum_ref)
    advance(j, now_ref, before_ref, force_in_ref, sum_ref, mass_ref, modes_ref, next_ref)
    front(j, next_ref, node_ref, elem_ref, place_ref, harmonic_ref, table_ref, deriv_ref,
          deriv_t_ref, radial_ref, shear_ref, partial_ref, force_ref, edge_ref)


def last_kernel(
    drive_ref, edge_in_ref, harmonic_ref, place_ref, now_ref, before_ref, force_in_ref,
    node_ref, elem_ref, mass_ref, modes_ref, box_ref, dest_ref,
    next_ref, box_out_ref, high_ref, low_ref, left_ref, sum_ref,
):
    j = lax.axis_index("box")
    slot_reactions(drive_ref, harmonic_ref, place_ref, edge_in_ref, high_ref, low_ref)
    scatter_slots(node_ref, elem_ref, high_ref, low_ref, left_ref, sum_ref)
    advance(j, now_ref, before_ref, force_in_ref, sum_ref, mass_ref, modes_ref, next_ref)
    box = box_ref[...]
    line = jnp.concatenate([box[m : m + 1, :] for m in range(8)], axis=1)
    pieces = jnp.concatenate([piece.astype(F32) for piece in split3(line)], axis=0).astype(BF16)
    for r in range(8):
        out = dot(pieces, hot(iota((1024, 128), 0) == dest_ref[r : r + 1, :]))
        box_out_ref[r : r + 1, :] = out[0:1] + (out[1:2] + out[2:3])


def exchange_kernel(
    last, partial_ref, spring_ref, mass_ref, weight_ref, now_ref, before_ref, edge_ref,
    drive_ref, next_ref, edge_out_ref,
    sums, drive, drives, edges, ways, returned,
    sum_send, sum_recv, drive_send, drive_recv, edge_send, edge_recv, way_send, way_recv,
):
    i = lax.axis_index("mer")
    j = lax.axis_index("box")
    above = lax.rem(i + 1, MER)
    below = lax.rem(i + MER - 1, MER)
    mer_peers = [lax.rem(i + o, MER) for o in range(1, MER)]
    box_peers = [lax.rem(j + o, BOX) for o in range(1, BOX)]
    met = mer_peers if last else [above, below]
    greet([(q, j) for q in met] + [(i, q) for q in box_peers])
    copies = []
    for o, q in enumerate(box_peers):
        copy = pltpu.make_async_remote_copy(
            src_ref=partial_ref.at[pl.ds(pl.multiple_of(q * 8, 8), 8), :],
            dst_ref=sums.at[o],
            send_sem=sum_send.at[o],
            recv_sem=sum_recv.at[o],
            device_id=(i, q),
            device_id_type=MESH,
        )
        copy.start()
        copies.append(copy)
    up = pltpu.make_async_remote_copy(
        src_ref=edge_ref.at[2:4], dst_ref=edges.at[0:2],
        send_sem=edge_send.at[0], recv_sem=edge_recv.at[0],
        device_id=(above, j), device_id_type=MESH,
    )
    down = pltpu.make_async_remote_copy(
        src_ref=edge_ref.at[0:2], dst_ref=edges.at[2:4],
        send_sem=edge_send.at[1], recv_sem=edge_recv.at[1],
        device_id=(below, j), device_id_type=MESH,
    )
    up.start()
    down.start()
    sample = partial_ref[pl.ds(pl.multiple_of(j * 8, 8), 8), :]
    for copy in copies:
        copy.wait()
    for o in range(BOX - 1):
        sample = sample + sums[o]
    now = now_ref[...]
    pull = spring_ref[...] * (sample - now)
    drive[...] = -weight_ref[...] * pull
    copies = []
    for o, q in enumerate(box_peers):
        copy = pltpu.make_async_remote_copy(
            src_ref=drive,
            dst_ref=drives.at[j],
            send_sem=drive_send.at[o],
            recv_sem=drive_recv.at[o],
            device_id=(i, q),
            device_id_type=MESH,
        )
        copy.start()
        copies.append(copy)
    after = 2.0 * now - before_ref[...] + STEP_SCALE * pull / mass_ref[...]
    if last:
        for m in range(8):
            ways[m] = jnp.broadcast_to(after[m : m + 1, :], (8, 128))
        for o, q in enumerate(mer_peers):
            copy = pltpu.make_async_remote_copy(
                src_ref=ways.at[q // 2],
                dst_ref=returned.at[i],
                send_sem=way_send.at[o],
                recv_sem=way_recv.at[o],
                device_id=(q, j),
                device_id_type=MESH,
            )
            copy.start()
            copies.append(copy)
        returned[i] = ways[i // 2]
    else:
        next_ref[...] = after
    drives[j] = drive[...]
    up.wait()
    down.wait()
    for g in range(4):
        ghost = (i == 0) if g < 2 else (i == MER - 1)
        edge_out_ref[g] = jnp.where(ghost, 0.0, edges[g])
    for copy in copies:
        copy.wait()
    if last:
        even = jnp.concatenate([returned[2 * r, 0:1, :] for r in range(8)], axis=0)
        odd = jnp.concatenate([returned[2 * r + 1, 0:1, :] for r in range(8)], axis=0)
        next_ref[...] = halves(even, odd, lax.rem(i, 2))
    for b in range(BOX):
        drive_ref[b * 8 : (b + 1) * 8, :] = drives[b]


def shape(*dims, dtype=F32):
    return jax.ShapeDtypeStruct(dims, dtype)


def call(kernel, outs, scratch, name, collective=None):
    params = dict(vmem_limit_bytes=48 << 20)
    if collective is not None:
        params.update(collective_id=collective, has_side_effects=True)
    return pl.pallas_call(
        kernel,
        out_shape=outs,
        scratch_shapes=scratch,
        compiler_params=pltpu.CompilerParams(**params),
        name=name,
    )


def dma(count):
    return pltpu.SemaphoreType.DMA((count,))


def exchange(last):
    return call(
        functools.partial(exchange_kernel, last),
        [shape(ROWS, 128), shape(8, 128), shape(4, COLS, 128)],
        [
            pltpu.VMEM((7, 8, 128), F32), pltpu.VMEM((8, 128), F32), pltpu.VMEM((8, 8, 128), F32),
            pltpu.VMEM((4, COLS, 128), F32), pltpu.VMEM((8, 8, 128), F32),
            pltpu.VMEM((MER, 8, 128), F32),
            dma(7), dma(7), dma(7), dma(7), dma(2), dma(2), dma(15), dma(15),
        ],
        "exchange_last" if last else "exchange",
        2 if last else 1,
    )


BACK_SCRATCH = [
    pltpu.VMEM((ALL_GROUPS, COLS, 128), BF16), pltpu.VMEM((ALL_GROUPS, COLS, 128), BF16),
    pltpu.VMEM((PAIRS * COLS, 512), BF16), pltpu.VMEM((PAIRS * COLS, 256), F32),
]


def per_device(
    annulus, annulus_prev, derivative, radial_modulus, shear_modulus, node_mass, element_modes,
    upper_rows, lower_rows, coupling_rows, coupling_target, box_field, box_prev, box_angle,
    box_spring, box_mass, box_weight, box_slot,
):
    flat = NODES * COLS
    now = annulus.reshape(flat, ELEMS)
    before = annulus_prev.reshape(flat, ELEMS)
    modes = element_modes.reshape(1, ELEMS)
    deriv_t = derivative.T

    send, dest, node, elem = call(
        setup_kernel,
        [shape(8, 8, 128), shape(8, 128, dtype=I32), shape(ALL_GROUPS, 128, dtype=I32),
         shape(ALL_GROUPS, 128, dtype=I32)],
        [pltpu.VMEM((8, 8, 128), F32)],
        "setup",
    )(
        *(x.reshape(8, 128) for x in (
            box_slot, box_angle, box_spring, box_mass, box_weight, box_field, box_prev)),
        coupling_rows.reshape(16, 128), coupling_target.reshape(16, 128),
        lower_rows.reshape(2, 128), upper_rows.reshape(2, 128),
    )
    own, angle, place = call(
        distribute_kernel,
        [shape(5, 8, 128), shape(ROWS, 128), shape(ROWS, 128, dtype=I32)],
        [
            pltpu.VMEM((MER, 8, 128), F32), pltpu.VMEM((2, 8, 128), F32),
            pltpu.VMEM((BOX, 2, 8, 128), F32), dma(15), dma(15), dma(7), dma(7),
        ],
        "distribute",
        0,
    )(send)
    spring, mass, weight, box_now, box_before = (own[k] for k in range(5))
    table = pltpu.VMEM((GROUPS, COLS, 128), F32)
    harmonic, partial, force, edge = call(
        first_kernel,
        [shape(ROWS, COLS, 128), shape(ROWS, 128), shape(flat, ELEMS), shape(4, COLS, 128)],
        [table],
        "first",
    )(angle, place, now, node, elem, derivative, deriv_t, radial_modulus, shear_modulus)
    drive, box_next, edge = exchange(False)(
        partial, spring, mass, weight, box_now, box_before, edge)
    later, partial, force, edge = call(
        middle_kernel,
        [shape(flat, ELEMS), shape(ROWS, 128), shape(flat, ELEMS), shape(4, COLS, 128)],
        [table] + BACK_SCRATCH,
        "middle",
    )(drive, edge, harmonic, place, now, before, force, node, elem, derivative, deriv_t,
      radial_modulus, shear_modulus, node_mass, modes)
    drive, box_back, edge = exchange(True)(
        partial, spring, mass, weight, box_next, box_now, edge)
    final, box_out = call(
        last_kernel, [shape(flat, ELEMS), shape(8, 128)], BACK_SCRATCH, "last"
    )(drive, edge, harmonic, place, later, now, force, node, elem, node_mass, modes, box_back, dest)
    return final.reshape(NODES, COLS, ELEMS), box_out.reshape(1024)


def solution(mesh):
    mer_box = P(("mer", "box"))
    in_specs = (
        P(None, "box", "mer"), P(None, "box", "mer"), P(),
        P(None, "mer"), P(None, "mer"), P(None, "mer"),
        P("mer"), P("mer"), P("mer"), P("mer"), P("mer", None),
        mer_box, mer_box, mer_box, mer_box, mer_box, mer_box, mer_box,
    )
    return jax.shard_map(
        per_device, mesh=mesh, in_specs=in_specs,
        out_specs=(P(None, "box", "mer"), mer_box), check_vma=False,
    )
```

profile of v0, /device:TPU:1, one launch (start us, length us, event | category | flops | bytes accessed | tf_op | source)
XLA Modules:
  0.0 128.6 jit_solution(7355300463617434254)
XLA Ops:
  0.6 0.8 copy.20
  1.4 0.7 copy-done.13
  2.1 0.7 copy-done.14
  2.8 0.7 copy-done.15
  3.5 0.7 copy-done.16
  4.2 0.7 copy-done.17
  9.0 2.5 %setup.1 = (f32[8,8,128]{2,1,0:T(8,128)S(1)}, s32[8,128]{1,0:T(8,128)S(1)}, s32[36,128]{1,0:T(8,128)S(1)}, s32[36,128]{1,0:T(8,128)S(1)}) custom-call(s32[8,128]{1,0:T(8,128)S(1)} %bitcast.35, f32[8,128]{1,0:T(8,128)S(1)} %bitcast.36, f32[8,128]{1,0:T(8,128)S(1)} %bitcast.37, f32[8,128]{1,0:T(8,128)S(1)} %bitcast.38, f32[8,128]{1,0:T(8,128)S(1)} %bitcast.39, ...), custom_call_target="tpu_custom_call" | custom-call | tf_op jit(solution)/shard_map/setup/pallas_call | solution.py:557
  11.5 17.2 %distribute.1 = (f32[5,8,128]{2,1,0:T(8,128)S(1)}, f32[64,128]{1,0:T(8,128)S(1)}, s32[64,128]{1,0:T(8,128)S(1)}) custom-call(f32[8,8,128]{2,1,0:T(8,128)S(1)} %get-tuple-element.25.send_ref), custom_call_target="tpu_custom_call" | custom-call | tf_op jit(solution)/shard_map/distribute/pallas_call | solution.py:569
  28.7 1.1 copy-done.2
  29.9 0.7 copy-done.6
  30.6 0.7 copy-done.8
  31.3 0.7 copy-done.10
  32.0 19.4 %first.1 = (f32[64,64,128]{2,1,0:T(8,128)S(1)}, f32[64,128]{1,0:T(8,128)S(1)}, f32[1600,128]{1,0:T(8,128)S(1)}, f32[4,64,128]{2,1,0:T(8,128)S(1)}) custom-call(f32[64,128]{1,0:T(8,128)S(1)} %get-tuple-element.26.angle_ref, s32[64,128]{1,0:T(8,128)S(1)} %get-tuple-element.27.place_ref, f32[1600,128]{1,0:T(8,128)S(1)} %bitcast.27, ...), custom_call_target="tpu_custom_call" | custom-call | tf_op jit(solution)/shard_map/first/pallas_call | solution.py:581
  51.4 1.4 %copy-done = f32[64,64,128]{2,1,0:T(8,128)} copy-done((f32[64,64,128]{2,1,0:T(8,128)}, f32[64,64,128]{2,1,0:T(8,128)S(1)}, u32[]{:S(2)}) %copy-start) | copy-done | bytes 2097176
  52.8 11.1 %exchange.1 = (f32[64,128]{1,0:T(8,128)S(1)}, f32[8,128]{1,0:T(8,128)S(1)}, f32[4,64,128]{2,1,0:T(8,128)S(1)}) custom-call(f32[64,128]{1,0:T(8,128)S(1)} %get-tuple-element.30.partial_ref, f32[8,128]{1,0:T(8,128)S(1)} %get-tuple-element.52.spring_ref, f32[8,128]{1,0:T(8,128)S(1)} %get-tuple-element.51.mass_ref, f32[8,128]{1,0:T(8,128)S(1)} %get-tuple-element.50.weight_ref, ...), custom_call_target="tpu_custom_call" | custom-call | tf_op jit(solution)/shard_map/exchange/pallas_call | solution.py:587
  63.9 1.1 copy-done.3
  65.0 1.1 copy-done.5
  66.2 0.7 copy-done.7
  66.9 0.7 copy-done.9
  67.6 0.7 copy-done.11
  68.3 0.7 copy-done.12
  69.7 33.0 %middle.1 = (f32[1600,128]{1,0:T(8,128)S(1)}, f32[64,128]{1,0:T(8,128)S(1)}, f32[1600,128]{1,0:T(8,128)S(1)}, f32[4,64,128]{2,1,0:T(8,128)S(1)}) custom-call(f32[64,128]{1,0:T(8,128)S(1)} %get-tuple-element.33.drive_ref, f32[4,64,128]{2,1,0:T(8,128)S(1)} %get-tuple-element.34.edge_in_ref, f32[64,64,128]{2,1,0:T(8,128)} %copy-done, ...), custom_call_target="tpu_custom_call" | custom-call | tf_op jit(solution)/shard_map/middle/pallas_call | solution.py:589
  102.7 10.7 %exchange_last.1 = (f32[64,128]{1,0:T(8,128)S(1)}, f32[8,128]{1,0:T(8,128)S(1)}, f32[4,64,128]{2,1,0:T(8,128)S(1)}) custom-call(f32[64,128]{1,0:T(8,128)S(1)} %get-tuple-element.37.partial_ref, f32[8,128]{1,0:T(8,128)S(1)} %get-tuple-element.52.spring_ref, f32[8,128]{1,0:T(8,128)S(1)} %get-tuple-element.51.mass_ref, ...), custom_call_target="tpu_custom_call" | custom-call | tf_op jit(solution)/shard_map/exchange_last/pallas_call | solution.py:596
  113.4 15.2 %last.1 = (f32[1600,128]{1,0:T(8,128)}, f32[8,128]{1,0:T(8,128)}) custom-call(f32[64,128]{1,0:T(8,128)S(1)} %get-tuple-element.40.drive_ref, f32[4,64,128]{2,1,0:T(8,128)S(1)} %get-tuple-element.41.edge_in_ref, f32[64,64,128]{2,1,0:T(8,128)S(1)} %copy-done.1, s32[64,128]{1,0:T(8,128)S(1)} %get-tuple-element.27.place_ref, ...), custom_call_target="tpu_custom_call" | custom-call | tf_op jit(solution)/shard_map/last/pallas_call | solution.py:598
  (35 shorter events, 4.8 us)
Async XLA Ops:
  1.4 0.7 copy-start.13
  2.1 0.7 copy-start.14
  2.8 0.7 copy-start.15
  3.5 0.7 copy-start.16
  4.2 0.7 copy-start.17
  4.9 0.7 copy-start.18
  5.6 0.7 copy-start.19
  6.3 0.7 copy-start.20
  7.0 0.7 copy-start.21
  7.6 0.7 copy-start.23
  8.3 0.7 copy-start.24
  28.7 1.1 copy-start.2
  29.9 0.7 copy-start.6
  30.6 0.7 copy-start.8
  31.3 0.7 copy-start.10
  51.4 1.4 %copy-start = (f32[64,64,128]{2,1,0:T(8,128)}, f32[64,64,128]{2,1,0:T(8,128)S(1)}, u32[]{:S(2)}) copy-start(f32[64,64,128]{2,1,0:T(8,128)S(1)} %get-tuple-element.35.harmonic_ref) | copy-start | bytes 6291460
  63.9 1.1 copy-start.3
  65.0 1.1 copy-start.5
  66.2 0.7 copy-start.7
  66.9 0.7 copy-start.9
  67.6 0.7 copy-start.11
  68.3 0.7 copy-start.12
  69.7 43.7 %copy-start.1 = (f32[64,64,128]{2,1,0:T(8,128)S(1)}, f32[64,64,128]{2,1,0:T(8,128)}, u32[]{:S(2)}) copy-start(f32[64,64,128]{2,1,0:T(8,128)} %copy-done) | copy-start | bytes 6291460
  69.7 43.7 %copy-start.4 = (f32[25,64,128]{2,1,0:T(8,128)S(1)}, f32[25,64,128]{2,1,0:T(8,128)}, u32[]{:S(2)}) copy-start(f32[25,64,128]{2,1,0:T(8,128)} %param.18) | copy-start | bytes 2457604
  (1 other events, 0.7 us)
where the time goes:
time: 130 us; the launch traced here: 129 us
  Pallas kernels  109 us (84%)
  local copies, waits for them, and re-layouts  18.8 us (14%)
    pallas_call x1, Pallas kernels, per_device(): call(middle_kernel, [shape(flat, ELEMS), shape(ROWS, 128), shape(flat, EL...  33 us
    pallas_call x1, Pallas kernels, per_device(): call(first_kernel, [shape(ROWS, COLS, 128), shape(ROWS, 128), shape(flat,...  19.4 us
    unnamed x51, local copies, waits for them, and re-layouts  18.8 us
    pallas_call x1, Pallas kernels, per_device(): call(distribute_kernel, [shape(5, 8, 128), shape(ROWS, 128), shape(ROWS,...  17.2 us
    pallas_call x1, Pallas kernels, per_device(): call(last_kernel, [shape(flat, ELEMS), shape(8, 128)], BACK_SCRATCH, 'last')  15.2 us
    pallas_call x1, Pallas kernels, per_device(): exchange(False)(partial, spring, mass, weight, box_now, box_before, edge)  11.1 us
    pallas_call x1, Pallas kernels, per_device(): exchange(True)(partial, spring, mass, weight, box_next, box_now, edge)  10.7 us

commit v1 on v0

v1 whole, which is shorter than its diff:
```python
import jax
import jax.numpy as jnp
from jax import lax
from jax.experimental import pallas as pl
from jax.experimental.pallas import tpu as pltpu
from jax.sharding import PartitionSpec as P

F32 = jnp.float32
BF16 = jnp.bfloat16
I32 = jnp.int32
MESH = pl.DeviceIdType.MESH

MER, BOX = 16, 8
MODES = 256
NODES, COLS, ELEMS = 25, 64, 128
PAIRS = 13
GROUPS = 32
ALL_GROUPS = 36
ROWS = 64
STEP_SCALE = 0.25


def iota(shape, dim):
    return lax.broadcasted_iota(I32, shape, dim)


def hot(mask):
    return jnp.where(mask, 1.0, 0.0).astype(BF16)


def dot(a, b):
    return jnp.dot(a, b, preferred_element_type=F32)


def dot_nt(a, b):
    return lax.dot_general(a, b, (((1,), (1,)), ((), ())), preferred_element_type=F32)


def split2(x):
    hi = x.astype(BF16)
    return hi, (x - hi.astype(F32)).astype(BF16)


def split3(x):
    hi = x.astype(BF16)
    rest = x - hi.astype(F32)
    mid = rest.astype(BF16)
    return hi, mid, (rest - mid.astype(F32)).astype(BF16)


def take_lanes(x, index):
    return jnp.take_along_axis(x, index, axis=1, mode="promise_in_bounds")


def sincos(x):
    k = jnp.floor(x * 0.6366197723675814 + 0.5)
    r = x - k * 1.5703125
    r = r - k * 4.837512969970703125e-4
    r = r - k * 7.54978995489188216e-8
    z = r * r
    s = ((-1.9515295891e-4 * z + 8.3321608736e-3) * z - 1.6666654611e-1) * z * r + r
    c = ((2.443315711809948e-5 * z - 1.388731625493765e-3) * z + 4.166664568298827e-2) * z * z
    c = c - 0.5 * z + 1.0
    q = k.astype(I32)
    odd = (q & 1) == 1
    sine = jnp.where(odd, c, s)
    cosine = jnp.where(odd, s, c)
    sine = jnp.where((q & 2) == 2, -sine, sine)
    cosine = jnp.where(((q + 1) & 2) == 2, -cosine, cosine)
    return sine, cosine


def before_lane():
    return hot(iota((128, 128), 0) < iota((128, 128), 1))


def order_nodes(sources, dest_ref, send_ref, fields):
    tri = before_lane()
    part = sources[1] & (MER - 1)
    values = [sources[0], (sources[1] >> 4).astype(F32)] + list(sources[2:])
    for r in range(8):
        for f in range(7):
            fields[r, f : f + 1, :] = values[f][r : r + 1, :]
        fields[r, 7:8, :] = jnp.zeros((1, 128), F32)
    base = jnp.zeros((MER, 1), F32)
    total = jnp.zeros((24, 1024), F32)
    for r in range(8):
        mine = part[r : r + 1, :]
        member = jnp.where(iota((MER, 128), 0) == mine, 1.0, 0.0)
        rank = dot(member.astype(BF16), tri) + base
        place = jnp.sum(member * rank, axis=0, keepdims=True).astype(I32)
        base = base + jnp.sum(member, axis=1, keepdims=True)
        dest = mine * 64 + place
        dest_ref[r : r + 1, :] = dest
        order = hot(iota((1024, 128), 0) == dest)
        pieces = jnp.concatenate(split3(fields[r]), axis=0)
        total = total + dot_nt(pieces, order)
    sorted_fields = total[0:8] + (total[8:16] + total[16:24])
    for m in range(8):
        send_ref[m] = sorted_fields[:, m * 128 : (m + 1) * 128]


def slot_table(rows, target, edges, node_ref, elem_ref):
    tri = before_lane()
    reader = (target & (BOX - 1)) * MER + (target >> 3)
    node1 = ((rows >> 7) + 1).astype(F32)
    elem = (rows & 127).astype(F32)
    count = jnp.zeros((128, 1), F32)
    table = jnp.zeros((64, 128), F32)
    for r in range(16):
        mine = reader[r : r + 1, :]
        member = jnp.where(iota((128, 128), 0) == mine, 1.0, 0.0)
        rank = dot(member.astype(BF16), tri) + count
        place = jnp.sum(member * rank, axis=0, keepdims=True).astype(I32)
        count = count + jnp.sum(member, axis=1, keepdims=True)
        lane = (mine & 3) * 32 + place
        group = iota((GROUPS, 128), 0) == (mine >> 2)
        values = jnp.concatenate(
            [
                jnp.where(group, jnp.broadcast_to(node1[r : r + 1, :], (GROUPS, 128)), 0.0),
                jnp.where(group, jnp.broadcast_to(elem[r : r + 1, :], (GROUPS, 128)), 0.0),
            ],
            axis=0,
        ).astype(BF16)
        table = table + dot_nt(values, hot(iota((128, 128), 0) == lane))
    node_ref[0:GROUPS, :] = table[0:GROUPS].astype(I32) - 1
    elem_ref[0:GROUPS, :] = table[GROUPS : 2 * GROUPS].astype(I32)
    for k, edge in enumerate(edges):
        node_ref[GROUPS + 2 * k : GROUPS + 2 * k + 2, :] = edge >> 7
        elem_ref[GROUPS + 2 * k : GROUPS + 2 * k + 2, :] = edge & 127


def halves(even, odd, half):
    low = jnp.where(half == 0, even, pltpu.roll(even, 64, 1))
    high = jnp.where(half == 1, odd, pltpu.roll(odd, 64, 1))
    return jnp.where(iota((8, 128), 1) < 64, low, high)


def harmonics(j, angles, block, harmonic_ref):
    sub = iota((8, 128), 0).astype(F32)
    first = (lax.rem(j, 4) * 64).astype(F32)
    is_sine = j >= 4
    for r in range(8):
        angle = jnp.broadcast_to(angles[r : r + 1, :], (8, 128))
        base_sin, base_cos = sincos(angle * (sub + first))
        step_sin, step_cos = sincos(angle * (sub * 8.0))
        a = jnp.where(is_sine, base_sin, base_cos)
        b = jnp.where(is_sine, -base_cos, base_sin)
        for t in range(8):
            harmonic_ref[block * 8 + r, t * 8 : (t + 1) * 8, :] = (
                a * step_cos[t : t + 1, :] - b * step_sin[t : t + 1, :]
            )


def gather_rows(values_ref, node, elem, groups):
    index = jnp.broadcast_to(elem, (8, 128))
    node = jnp.broadcast_to(node, (8, 128))
    acc = [jnp.zeros((8, 128), F32) for _ in range(8)]
    for a in range(NODES):
        mask = node == a
        for c in range(8):
            taken = take_lanes(values_ref[a * 64 + c * 8 : a * 64 + c * 8 + 8, :], index)
            acc[c] = jnp.where(mask, taken, acc[c])
    return acc


def fill_table(values_ref, node_ref, elem_ref, table_ref):
    def body(g, carry):
        acc = gather_rows(values_ref, node_ref[pl.ds(g, 1), :], elem_ref[pl.ds(g, 1), :], 1)
        for c in range(8):
            table_ref[g, c * 8 : (c + 1) * 8, :] = acc[c]
        return carry

    lax.fori_loop(0, GROUPS, body, 0)


def node_lane(place, odd):
    return place + (iota((1, 128), 1) >> 6) * 32 + odd * 64


def sample_nodes(table_ref, places, block, harmonic_ref):
    rows = []
    for r in range(8):
        index = jnp.broadcast_to(node_lane(places[r : r + 1, :], r % 2), (8, 128))
        group = block * 4 + r // 2
        acc = jnp.zeros((8, 128), F32)
        for c in range(8):
            taken = take_lanes(table_ref[group, c * 8 : (c + 1) * 8, :], index)
            acc = acc + taken * harmonic_ref[block * 8 + r, c * 8 : (c + 1) * 8, :]
        rows.append(jnp.sum(acc, axis=0, keepdims=True))
    return jnp.concatenate(rows, axis=0)


def compute_force(j, values_ref, deriv_ref, radial_ref, shear_ref, force_ref):
    deriv = deriv_ref[...]
    radial = radial_ref[...]
    shear = shear_ref[...]
    first = lax.rem(j, 4) * 64

    def body(k, carry):
        x = jnp.concatenate(
            [values_ref[pl.ds(k * 8 + c, NODES, stride=64), :] for c in range(8)], axis=1
        )
        gradient = jnp.dot(deriv, x, precision=lax.Precision.HIGHEST, preferred_element_type=F32)
        flux = gradient * jnp.concatenate([radial] * 8, axis=1)
        back = lax.dot_general(
            deriv, flux, (((0,), (0,)), ((), ())),
            precision=lax.Precision.HIGHEST, preferred_element_type=F32,
        )
        for c in range(8):
            wave = (first + k * 8 + c).astype(F32) * (2.0 / MODES)
            lanes = slice(c * 128, (c + 1) * 128)
            force_ref[pl.ds(k * 8 + c, NODES, stride=64), :] = (
                -back[:, lanes] - shear * (wave * wave) * x[:, lanes]
            )
        return carry

    lax.fori_loop(0, 8, body, 0)


def edge_forces(force_ref, node_ref, elem_ref, edge_ref):
    def body(g, carry):
        acc = gather_rows(
            force_ref, node_ref[pl.ds(GROUPS + g, 1), :], elem_ref[pl.ds(GROUPS + g, 1), :], 1
        )
        for c in range(8):
            edge_ref[g, c * 8 : (c + 1) * 8, :] = acc[c]
        return carry

    lax.fori_loop(0, 4, body, 0)


def slot_reactions(drives, places, block, harmonic_ref, high_ref, low_ref):
    for k in range(4):
        pieces, hots = [], []
        for odd in range(2):
            r = 2 * k + odd
            x = harmonic_ref[block * 8 + r] * drives[r : r + 1, :]
            pieces.append(split2(x))
            lane = node_lane(places[r : r + 1, :], odd)
            hots.append(hot(iota((128, 128), 0) == lane))
        left = jnp.concatenate([pieces[0][0], pieces[1][0], pieces[0][1], pieces[1][1]], axis=1)
        right = jnp.concatenate(hots + hots, axis=1)
        high, low = split2(dot_nt(left, right))
        high_ref[block * 4 + k] = high
        low_ref[block * 4 + k] = low


def scatter_slots(first, node_ref, elem_ref, high_ref, low_ref, left_ref, sum_ref):
    def body(t, carry):
        hots = []
        for h in range(2):
            g = 2 * t + h
            node = node_ref[pl.ds(g, 1), :]
            lane = (node & 1) * 128 + elem_ref[pl.ds(g, 1), :]
            hots.append(hot(iota((256, 128), 0) == lane))
            pair = node >> 1
            high = high_ref[g]
            low = low_ref[g]
            for a in range(PAIRS):
                mask = jnp.broadcast_to(hot(pair == a), (COLS, 128))
                left_ref[a * 64 : (a + 1) * 64, h * 128 : (h + 1) * 128] = high * mask
                left_ref[a * 64 : (a + 1) * 64, 256 + h * 128 : 384 + h * 128] = low * mask
        right = jnp.concatenate(hots + hots, axis=1)
        sum_ref[...] += dot_nt(left_ref[...], right)
        return carry

    lax.fori_loop(first, first + 2, body, 0)


def advance(j, now_ref, before_ref, force_ref, sum_ref, mass_ref, modes_ref, next_ref):
    order = lax.rem(j, 4) * 64 + iota((COLS, 128), 0)
    live = jnp.where(order < modes_ref[...], STEP_SCALE, 0.0)
    for a in range(NODES):
        rows = slice(a * 64, (a + 1) * 64)
        pair = a // 2
        lanes = slice((a % 2) * 128, (a % 2) * 128 + 128)
        total = force_ref[rows, :] + sum_ref[pair * 64 : (pair + 1) * 64, lanes]
        next_ref[rows, :] = (
            2.0 * now_ref[rows, :] - before_ref[rows, :] + live * total / mass_ref[a : a + 1, :]
        )


INPUTS = 18


def whole_kernel(*refs):
    hbm = refs[:INPUTS]
    out_ref, box_out_ref = refs[INPUTS : INPUTS + 2]
    vmem = refs[INPUTS + 2 : 2 * INPUTS + 2]
    (
        fields, dest_ref, send_ref, node_ref, elem_ref, received, share, shared, harmonic_ref,
        table_ref, force_ref, next_ref, last_ref, high_ref, low_ref, left_ref, sum_ref,
        edge_ref, edges, partial, sums, drive, drives, ways, returned, box_last,
        load_sem, send_sem, recv_sem, share_send, share_recv, edge_send, edge_recv,
        sum_send, sum_recv, drive_send, drive_recv, way_send, way_recv, out_sem,
    ) = refs[2 * INPUTS + 2 :]
    (
        angle_ref, slot_ref, spring_ref, mass_ref, weight_ref, now_ref, before_ref,
        rows_ref, target_ref, lower_ref, upper_ref, value_ref, old_ref, deriv_ref,
        radial_ref, shear_ref, node_mass_ref, modes_ref,
    ) = vmem
    i = lax.axis_index("mer")
    j = lax.axis_index("box")
    above = lax.rem(i + 1, MER)
    below = lax.rem(i + MER - 1, MER)

    loads = [pltpu.make_async_copy(hbm[k], vmem[k], load_sem.at[k]) for k in range(INPUTS)]
    for load in loads:
        load.start()
    barrier = pltpu.get_barrier_semaphore()
    for o in range(1, MER):
        pl.semaphore_signal(
            barrier, inc=1, device_id=(lax.rem(i + o, MER), j), device_id_type=MESH)
    for o in range(1, BOX):
        pl.semaphore_signal(
            barrier, inc=1, device_id=(i, lax.rem(j + o, BOX)), device_id_type=MESH)

    def way(source, target, send, recv, device):
        return pltpu.make_async_remote_copy(
            src_ref=source, dst_ref=target, send_sem=send, recv_sem=recv,
            device_id=device, device_id_type=MESH)

    def to_part(o):
        q = lax.rem(i + o, MER)
        return way(send_ref.at[lax.div(q, 2)], received.at[i], send_sem.at[o], recv_sem.at[o], (q, j))

    def to_share(o):
        q = lax.rem(j + o, BOX)
        return way(share, shared.at[j], share_send.at[o], share_recv.at[o], (i, q))

    def to_sum(step, o):
        q = lax.rem(j + BOX - o, BOX)
        return way(partial.at[step, q], sums.at[step, o],
                   sum_send.at[step, o], sum_recv.at[step, o], (i, q))

    def to_drive(step, o):
        q = lax.rem(j + o, BOX)
        return way(drive.at[step], drives.at[step, j],
                   drive_send.at[step, o], drive_recv.at[step, o], (i, q))

    def to_back(o):
        q = lax.rem(i + o, MER)
        return way(ways.at[lax.div(q, 2)], returned.at[i], way_send.at[o], way_recv.at[o], (q, j))

    def to_edges(step):
        return (
            way(edge_ref.at[step, 2:4], edges.at[step, 0:2],
                edge_send.at[step, 0], edge_recv.at[step, 0], (above, j)),
            way(edge_ref.at[step, 0:2], edges.at[step, 2:4],
                edge_send.at[step, 1], edge_recv.at[step, 1], (below, j)),
        )

    def repeat(first, last, work):
        def body(o, carry):
            work(o)
            return carry

        lax.fori_loop(first, last, body, 0)

    for load in loads[:7]:
        load.wait()
    order_nodes([ref[...] for ref in vmem[:7]], dest_ref, send_ref, fields)
    pl.semaphore_wait(barrier, MER + BOX - 2)
    repeat(1, MER, lambda o: to_part(o).start())
    received[i] = send_ref[lax.div(i, 2)]
    for load in loads[7:]:
        load.wait()
    slot_table(rows_ref[...], target_ref[...], (lower_ref[...], upper_ref[...]), node_ref, elem_ref)
    fill_table(value_ref, node_ref, elem_ref, table_ref)

    repeat(1, MER, lambda o: to_part(o).wait_recv())
    half = lax.rem(i, 2)
    own = []
    for f in range(7):
        even = jnp.concatenate([received[2 * r, f : f + 1, :] for r in range(8)], axis=0)
        odd = jnp.concatenate([received[2 * r + 1, f : f + 1, :] for r in range(8)], axis=0)
        own.append(halves(even, odd, half))
    share[0] = own[0]
    share[1] = own[1]
    repeat(1, BOX, lambda o: to_share(o).start())
    shared[j] = share[...]
    spring, mass, weight, box_now, box_before = own[2:]

    def forces(step, ref):
        compute_force(j, ref, deriv_ref, radial_ref, shear_ref, force_ref)
        edge_forces(force_ref, node_ref, elem_ref, edge_ref.at[step])
        for copy in to_edges(step):
            copy.start()

    def sample_block(step, block):
        partial[step, block] = sample_nodes(
            table_ref, shared[block, 1].astype(I32), block, harmonic_ref)

    def pulls(step, now):
        sample = partial[step, j]
        for o in range(1, BOX):
            to_sum(step, o).wait_recv()
            sample = sample + sums[step, o]
        pull = spring * (sample - now)
        drive[step] = -weight * pull
        repeat(1, BOX, lambda o: to_drive(step, o).start())
        drives[step, j] = drive[step]
        return pull

    def react(step, block):
        slot_reactions(drives[step, block], shared[block, 1].astype(I32), block,
                       harmonic_ref, high_ref, low_ref)
        scatter_slots(block * 2, node_ref, elem_ref, high_ref, low_ref, left_ref, sum_ref)

    def reactions(step):
        sum_ref[...] = jnp.zeros_like(sum_ref)
        react(step, j)

        def work(o):
            to_drive(step, o).wait_recv()
            react(step, lax.rem(j + BOX - o, BOX))

        repeat(1, BOX, work)
        for copy in to_edges(step):
            copy.wait_recv()
        for g in range(4):
            ghost = (i == 0) if g < 2 else (i == MER - 1)
            high, low = split2(jnp.where(ghost, 0.0, edges[step, g]))
            high_ref[GROUPS + g] = high
            low_ref[GROUPS + g] = low
        scatter_slots(GROUPS // 2, node_ref, elem_ref, high_ref, low_ref, left_ref, sum_ref)

    forces(0, value_ref)

    def enter(block):
        harmonics(j, shared[block, 0], block, harmonic_ref)
        sample_block(0, block)

    enter(j)

    def enter_peer(o):
        to_share(o).wait_recv()
        enter(lax.rem(j + BOX - o, BOX))
        to_sum(0, o).start()

    repeat(1, BOX, enter_peer)
    pull = pulls(0, box_now)
    box_next = 2.0 * box_now - box_before + STEP_SCALE * pull / mass
    reactions(0)
    advance(j, value_ref, old_ref, force_ref, sum_ref, node_mass_ref, modes_ref, next_ref)

    fill_table(next_ref, node_ref, elem_ref, table_ref)

    def sample_peer(o):
        sample_block(1, lax.rem(j + BOX - o, BOX))
        to_sum(1, o).start()

    repeat(1, BOX, sample_peer)
    sample_block(1, j)
    forces(1, next_ref)
    pull = pulls(1, box_next)
    box_after = 2.0 * box_next - box_now + STEP_SCALE * pull / mass
    for m in range(8):
        ways[m] = jnp.broadcast_to(box_after[m : m + 1, :], (8, 128))
    repeat(1, MER, lambda o: to_back(o).start())
    returned[i] = ways[lax.div(i, 2)]
    reactions(1)
    advance(j, next_ref, value_ref, force_ref, sum_ref, node_mass_ref, modes_ref, last_ref)
    result = pltpu.make_async_copy(last_ref, out_ref, out_sem.at[0])
    result.start()

    repeat(1, MER, lambda o: to_back(o).wait_recv())
    even = jnp.concatenate([returned[2 * r, 0:1, :] for r in range(8)], axis=0)
    odd = jnp.concatenate([returned[2 * r + 1, 0:1, :] for r in range(8)], axis=0)
    box = halves(even, odd, half)
    line = jnp.concatenate([box[m : m + 1, :] for m in range(8)], axis=1)
    pieces = jnp.concatenate([piece.astype(F32) for piece in split3(line)], axis=0).astype(BF16)
    for r in range(8):
        out = dot(pieces, hot(iota((1024, 128), 0) == dest_ref[r : r + 1, :]))
        box_last[r : r + 1, :] = out[0:1] + (out[1:2] + out[2:3])
    box_result = pltpu.make_async_copy(box_last, box_out_ref, out_sem.at[1])
    box_result.start()

    def sent(o):
        to_share(o).wait_send()
        for step in range(2):
            to_sum(step, o).wait_send()
            to_drive(step, o).wait_send()

    repeat(1, BOX, sent)

    def sent_far(o):
        to_part(o).wait_send()
        to_back(o).wait_send()

    repeat(1, MER, sent_far)
    for step in range(2):
        for copy in to_edges(step):
            copy.wait_send()
    result.wait()
    box_result.wait()


def per_device(
    annulus, annulus_prev, derivative, radial_modulus, shear_modulus, node_mass, element_modes,
    upper_rows, lower_rows, coupling_rows, coupling_target, box_field, box_prev, box_angle,
    box_spring, box_mass, box_weight, box_slot,
):
    flat = NODES * COLS
    args = [
        x.reshape(8, 128)
        for x in (box_angle, box_slot, box_spring, box_mass, box_weight, box_field, box_prev)
    ] + [
        coupling_rows.reshape(16, 128), coupling_target.reshape(16, 128),
        lower_rows.reshape(2, 128), upper_rows.reshape(2, 128),
        annulus.reshape(flat, ELEMS), annulus_prev.reshape(flat, ELEMS), derivative,
        radial_modulus, shear_modulus, node_mass, element_modes.reshape(1, ELEMS),
    ]
    vmem = pltpu.VMEM
    scratch = [vmem(x.shape, x.dtype) for x in args] + [
        vmem((8, 8, 128), F32),
        vmem((8, 128), I32),
        vmem((8, 8, 128), F32),
        vmem((ALL_GROUPS, 128), I32),
        vmem((ALL_GROUPS, 128), I32),
        vmem((MER, 8, 128), F32),
        vmem((2, 8, 128), F32),
        vmem((BOX, 2, 8, 128), F32),
        vmem((ROWS, COLS, 128), F32),
        vmem((GROUPS, COLS, 128), F32),
        vmem((flat, ELEMS), F32),
        vmem((flat, ELEMS), F32),
        vmem((flat, ELEMS), F32),
        vmem((ALL_GROUPS, COLS, 128), BF16),
        vmem((ALL_GROUPS, COLS, 128), BF16),
        vmem((PAIRS * COLS, 512), BF16),
        vmem((PAIRS * COLS, 256), F32),
        vmem((2, 4, COLS, 128), F32),
        vmem((2, 4, COLS, 128), F32),
        vmem((2, BOX, 8, 128), F32),
        vmem((2, BOX, 8, 128), F32),
        vmem((2, 8, 128), F32),
        vmem((2, BOX, 8, 128), F32),
        vmem((8, 8, 128), F32),
        vmem((MER, 8, 128), F32),
        vmem((8, 128), F32),
    ]
    dma = pltpu.SemaphoreType.DMA
    scratch += [dma((INPUTS,))] + [dma((MER,))] * 2 + [dma((BOX,))] * 2 + [dma((2, 2))] * 2
    scratch += [dma((2, BOX))] * 4 + [dma((MER,))] * 2 + [dma((2,))]
    any_space = pl.BlockSpec(memory_space=pl.ANY)
    final, box_out = pl.pallas_call(
        whole_kernel,
        out_shape=[jax.ShapeDtypeStruct((flat, ELEMS), F32), jax.ShapeDtypeStruct((8, 128), F32)],
        in_specs=[any_space] * INPUTS,
        out_specs=[any_space] * 2,
        scratch_shapes=scratch,
        compiler_params=pltpu.CompilerParams(
            vmem_limit_bytes=56 << 20, collective_id=0, has_side_effects=True),
        name="coupled_steps",
    )(*args)
    return final.reshape(NODES, COLS, ELEMS), box_out.reshape(1024)


def solution(mesh):
    mer_box = P(("mer", "box"))
    in_specs = (
        P(None, "box", "mer"), P(None, "box", "mer"), P(),
        P(None, "mer"), P(None, "mer"), P(None, "mer"),
        P("mer"), P("mer"), P("mer"), P("mer"), P("mer", None),
        mer_box, mer_box, mer_box, mer_box, mer_box, mer_box, mer_box,
    )
    return jax.shard_map(
        per_device, mesh=mesh, in_specs=in_specs,
        out_specs=(P(None, "box", "mer"), mer_box), check_vma=False,
    )
```

time: 130 us -> 73.1 us (0.56)
  Pallas kernels: 109 us -> 69.5 us
  local copies, waits for them, and re-layouts: 18.8 us -> 2.72 us
    pallas_call x7 -> x1, Pallas kernels: 109 us -> 69.5 us  [per_device(): pl.pallas_call(whole_kernel, out_shape=[jax.ShapeDtypeStruct((flat, ELEMS...]
    unnamed x51 -> x4, local copies, waits for them, and re-layouts: 18.8 us -> 2.72 us
where the time goes in v1:
time: 73.1 us; the launch traced here: 72.9 us
  Pallas kernels  69.5 us (95%)
  local copies, waits for them, and re-layouts  2.72 us (4%)
    pallas_call x1, Pallas kernels, per_device(): pl.pallas_call(whole_kernel, out_shape=[jax.ShapeDtypeStruct((flat, ELEMS...  69.5 us
    unnamed x4, local copies, waits for them, and re-layouts  2.72 us

profile of v1, /device:TPU:1, one launch (start us, length us, event | category | flops | bytes accessed | tf_op | source)
XLA Modules:
  0.0 72.9 jit_solution(12094539221646102624)
XLA Ops:
  0.6 69.5 %coupled_steps.1 = (f32[1600,128]{1,0:T(8,128)}, f32[8,128]{1,0:T(8,128)}) custom-call(f32[8,128]{1,0:T(8,128)} %bitcast.21, s32[8,128]{1,0:T(8,128)} %bitcast.22, f32[8,128]{1,0:T(8,128)} %bitcast.23, f32[8,128]{1,0:T(8,128)} %bitcast.24, f32[8,128]{1,0:T(8,128)} %bitcast.25, f32[8,128]{1,0:T(8,128)} %bitcast.26, f32[8,128]{1,0:T(8,128)} %bitcast.27, ...), custom_call_target="tpu_custom_call" | custom-call | tf_op jit(solution)/shard_map/coupled_steps/pallas_call | solution.py:548
  70.2 0.0 copy-start
  70.2 2.1 %copy.22 = f32[25,64,128]{2,1,0:T(8,128)} copy(f32[25,64,128]{2,1,0:T(8,128)} %bitcast.18) | data formatting | bytes 1638400
  72.3 0.0 copy-done
  72.3 0.6 copy.23
Async XLA Ops:
  70.2 2.1 %copy-start = (f32[8,128]{1,0:T(8,128)S(1)}, f32[8,128]{1,0:T(8,128)}, u32[]{:S(2)}) copy-start(f32[8,128]{1,0:T(8,128)} %get-tuple-element.5) | copy-start | bytes 12292

commit v2 on v1

--- a/solution.py
+++ b/solution.py
@@ -152,7 +152,7 @@
             )
 
 
-def gather_rows(values_ref, node, elem, groups):
+def gather_rows(values_ref, node, elem):
     index = jnp.broadcast_to(elem, (8, 128))
     node = jnp.broadcast_to(node, (8, 128))
     acc = [jnp.zeros((8, 128), F32) for _ in range(8)]
@@ -164,14 +164,47 @@
     return acc
 
 
-def fill_table(values_ref, node_ref, elem_ref, table_ref):
+MATRIX_GROUPS, LANE_GROUPS = 6, 2
+
+
+def keep_pieces(values, a, pieces_ref):
+    rows = slice((a // 2) * 64, (a // 2) * 64 + 64)
+    lane = (a % 2) * 128
+    high, low = split2(values)
+    pieces_ref[rows, lane : lane + 128] = high
+    pieces_ref[rows, 256 + lane : 384 + lane] = low
+
+
+def slot_hots(node_ref, elem_ref, hot_ref):
     def body(g, carry):
-        acc = gather_rows(values_ref, node_ref[pl.ds(g, 1), :], elem_ref[pl.ds(g, 1), :], 1)
-        for c in range(8):
-            table_ref[g, c * 8 : (c + 1) * 8, :] = acc[c]
+        lane = (node_ref[pl.ds(g, 1), :] & 1) * 128 + elem_ref[pl.ds(g, 1), :]
+        hot_ref[g] = hot(iota((256, 128), 0) == lane)
         return carry
 
-    lax.fori_loop(0, GROUPS, body, 0)
+    lax.fori_loop(0, ALL_GROUPS, body, 0)
+
+
+def fill_table(values_ref, pieces_ref, hot_ref, node_ref, elem_ref, table_ref):
+    def body(t, carry):
+        first = t * (MATRIX_GROUPS + LANE_GROUPS)
+        right = jnp.concatenate([hot_ref[first + k] for k in range(MATRIX_GROUPS)], axis=1)
+        out = dot(pieces_ref[...], jnp.concatenate([right, right], axis=0))
+        for k in range(LANE_GROUPS):
+            g = first + MATRIX_GROUPS + k
+            acc = gather_rows(values_ref, node_ref[pl.ds(g, 1), :], elem_ref[pl.ds(g, 1), :])
+            for c in range(8):
+                table_ref[g, c * 8 : (c + 1) * 8, :] = acc[c]
+        for k in range(MATRIX_GROUPS):
+            g = first + k
+            pair = node_ref[pl.ds(g, 1), :] >> 1
+            acc = jnp.zeros((COLS, 128), F32)
+            for a in range(PAIRS):
+                acc = jnp.where(
+                    pair == a, out[a * 64 : (a + 1) * 64, k * 128 : (k + 1) * 128], acc)
+            table_ref[g] = acc
+        return carry
+
+    lax.fori_loop(0, GROUPS // (MATRIX_GROUPS + LANE_GROUPS), body, 0)
 
 
 def node_lane(place, odd):
@@ -191,37 +224,44 @@
     return jnp.concatenate(rows, axis=0)
 
 
+def small_stack(matrix):
+    high, low = split2(matrix)
+    return jnp.concatenate([high, high, low], axis=1)
+
+
 def compute_force(j, values_ref, deriv_ref, radial_ref, shear_ref, force_ref):
     deriv = deriv_ref[...]
-    radial = radial_ref[...]
+    stack = small_stack(deriv[0:32, 0:32])
+    stack_t = small_stack(deriv.T[0:32, 0:32])
+    radial = jnp.concatenate([radial_ref[...], jnp.zeros((7, 128), F32)], axis=0)
+    radial = jnp.concatenate([radial] * 16, axis=1)
     shear = shear_ref[...]
     first = lax.rem(j, 4) * 64
 
+    def times(left, x):
+        high, low = split2(x)
+        return dot(left, jnp.concatenate([high, low, high], axis=0))
+
     def body(k, carry):
         x = jnp.concatenate(
-            [values_ref[pl.ds(k * 8 + c, NODES, stride=64), :] for c in range(8)], axis=1
+            [values_ref[pl.ds(k * 16 + c, 32, stride=64), :] for c in range(16)], axis=1
         )
-        gradient = jnp.dot(deriv, x, precision=lax.Precision.HIGHEST, preferred_element_type=F32)
-        flux = gradient * jnp.concatenate([radial] * 8, axis=1)
-        back = lax.dot_general(
-            deriv, flux, (((0,), (0,)), ((), ())),
-            precision=lax.Precision.HIGHEST, preferred_element_type=F32,
-        )
-        for c in range(8):
-            wave = (first + k * 8 + c).astype(F32) * (2.0 / MODES)
+        back = times(stack_t, times(stack, x) * radial)
+        for c in range(16):
+            wave = (first + k * 16 + c).astype(F32) * (2.0 / MODES)
             lanes = slice(c * 128, (c + 1) * 128)
-            force_ref[pl.ds(k * 8 + c, NODES, stride=64), :] = (
-                -back[:, lanes] - shear * (wave * wave) * x[:, lanes]
+            force_ref[pl.ds(k * 16 + c, NODES, stride=64), :] = (
+                -back[0:NODES, lanes] - shear * (wave * wave) * x[0:NODES, lanes]
             )
         return carry
 
-    lax.fori_loop(0, 8, body, 0)
+    lax.fori_loop(0, 4, body, 0)
 
 
 def edge_forces(force_ref, node_ref, elem_ref, edge_ref):
     def body(g, carry):
         acc = gather_rows(
-            force_ref, node_ref[pl.ds(GROUPS + g, 1), :], elem_ref[pl.ds(GROUPS + g, 1), :], 1
+            force_ref, node_ref[pl.ds(GROUPS + g, 1), :], elem_ref[pl.ds(GROUPS + g, 1), :]
         )
         for c in range(8):
             edge_ref[g, c * 8 : (c + 1) * 8, :] = acc[c]
@@ -246,29 +286,23 @@
         low_ref[block * 4 + k] = low
 
 
-def scatter_slots(first, node_ref, elem_ref, high_ref, low_ref, left_ref, sum_ref):
-    def body(t, carry):
-        hots = []
-        for h in range(2):
-            g = 2 * t + h
-            node = node_ref[pl.ds(g, 1), :]
-            lane = (node & 1) * 128 + elem_ref[pl.ds(g, 1), :]
-            hots.append(hot(iota((256, 128), 0) == lane))
-            pair = node >> 1
-            high = high_ref[g]
-            low = low_ref[g]
-            for a in range(PAIRS):
-                mask = jnp.broadcast_to(hot(pair == a), (COLS, 128))
-                left_ref[a * 64 : (a + 1) * 64, h * 128 : (h + 1) * 128] = high * mask
-                left_ref[a * 64 : (a + 1) * 64, 256 + h * 128 : 384 + h * 128] = low * mask
-        right = jnp.concatenate(hots + hots, axis=1)
-        sum_ref[...] += dot_nt(left_ref[...], right)
-        return carry
-
-    lax.fori_loop(first, first + 2, body, 0)
-
-
-def advance(j, now_ref, before_ref, force_ref, sum_ref, mass_ref, modes_ref, next_ref):
+def scatter_slots(first, node_ref, hot_ref, high_ref, low_ref, left_ref, sum_ref):
+    rights = []
+    for h in range(4):
+        pair = node_ref[pl.ds(first + h, 1), :] >> 1
+        high = high_ref[first + h]
+        low = low_ref[first + h]
+        for a in range(PAIRS):
+            mask = jnp.broadcast_to(hot(pair == a), (COLS, 128))
+            rows = slice(a * 64, (a + 1) * 64)
+            left_ref[rows, h * 128 : (h + 1) * 128] = high * mask
+            left_ref[rows, 512 + h * 128 : 640 + h * 128] = low * mask
+        rights.append(hot_ref[first + h])
+    sum_ref[...] += dot_nt(left_ref[...], jnp.concatenate(rights + rights, axis=1))
+
+
+def advance(j, now_ref, before_ref, force_ref, sum_ref, mass_ref, modes_ref, next_ref,
+            pieces_ref=None):
     order = lax.rem(j, 4) * 64 + iota((COLS, 128), 0)
     live = jnp.where(order < modes_ref[...], STEP_SCALE, 0.0)
     for a in range(NODES):
@@ -276,12 +310,15 @@
         pair = a // 2
         lanes = slice((a % 2) * 128, (a % 2) * 128 + 128)
         total = force_ref[rows, :] + sum_ref[pair * 64 : (pair + 1) * 64, lanes]
-        next_ref[rows, :] = (
-            2.0 * now_ref[rows, :] - before_ref[rows, :] + live * total / mass_ref[a : a + 1, :]
-        )
+        after = 2.0 * now_ref[rows, :] - before_ref[rows, :] + live * total / mass_ref[a : a + 1, :]
+        next_ref[rows, :] = after
+        if pieces_ref is not None:
+            keep_pieces(after, a, pieces_ref)
 
 
 INPUTS = 18
+VALUES = 11
+PADDED = 32 * COLS
 
 
 def whole_kernel(*refs):
@@ -292,6 +329,7 @@
         fields, dest_ref, send_ref, node_ref, elem_ref, received, share, shared, harmonic_ref,
         table_ref, force_ref, next_ref, last_ref, high_ref, low_ref, left_ref, sum_ref,
         edge_ref, edges, partial, sums, drive, drives, ways, returned, box_last,
+        pieces_ref, hot_ref, square_ref,
         load_sem, send_sem, recv_sem, share_send, share_recv, edge_send, edge_recv,
         sum_send, sum_recv, drive_send, drive_recv, way_send, way_recv, out_sem,
     ) = refs[2 * INPUTS + 2 :]
@@ -305,7 +343,12 @@
     above = lax.rem(i + 1, MER)
     below = lax.rem(i + MER - 1, MER)
 
-    loads = [pltpu.make_async_copy(hbm[k], vmem[k], load_sem.at[k]) for k in range(INPUTS)]
+    def landing(k):
+        if k == VALUES:
+            return value_ref.at[0 : NODES * COLS]
+        return vmem[k]
+
+    loads = [pltpu.make_async_copy(hbm[k], landing(k), load_sem.at[k]) for k in range(INPUTS)]
     for load in loads:
         load.start()
     barrier = pltpu.get_barrier_semaphore()
@@ -367,7 +410,17 @@
     for load in loads[7:]:
         load.wait()
     slot_table(rows_ref[...], target_ref[...], (lower_ref[...], upper_ref[...]), node_ref, elem_ref)
-    fill_table(value_ref, node_ref, elem_ref, table_ref)
+    slot_hots(node_ref, elem_ref, hot_ref)
+    square_ref[...] = jnp.zeros_like(square_ref)
+    square_ref[0:NODES, 0:NODES] = deriv_ref[...]
+    for ref in (value_ref, next_ref):
+        ref[NODES * COLS : PADDED, :] = jnp.zeros((PADDED - NODES * COLS, ELEMS), F32)
+    for a in range(NODES):
+        keep_pieces(value_ref[a * COLS : (a + 1) * COLS, :], a, pieces_ref)
+    for lane in (128, 384):
+        pieces_ref[(PAIRS - 1) * COLS : PAIRS * COLS, lane : lane + 128] = jnp.zeros(
+            (COLS, 128), BF16)
+    fill_table(value_ref, pieces_ref, hot_ref, node_ref, elem_ref, table_ref)
 
     repeat(1, MER, lambda o: to_part(o).wait_recv())
     half = lax.rem(i, 2)
@@ -383,7 +436,7 @@
     spring, mass, weight, box_now, box_before = own[2:]
 
     def forces(step, ref):
-        compute_force(j, ref, deriv_ref, radial_ref, shear_ref, force_ref)
+        compute_force(j, ref, square_ref, radial_ref, shear_ref, force_ref)
         edge_forces(force_ref, node_ref, elem_ref, edge_ref.at[step])
         for copy in to_edges(step):
             copy.start()
@@ -406,7 +459,7 @@
     def react(step, block):
         slot_reactions(drives[step, block], shared[block, 1].astype(I32), block,
                        harmonic_ref, high_ref, low_ref)
-        scatter_slots(block * 2, node_ref, elem_ref, high_ref, low_ref, left_ref, sum_ref)
+        scatter_slots(block * 4, node_ref, hot_ref, high_ref, low_ref, left_ref, sum_ref)
 
     def reactions(step):
         sum_ref[...] = jnp.zeros_like(sum_ref)
@@ -424,7 +477,7 @@
             high, low = split2(jnp.where(ghost, 0.0, edges[step, g]))
             high_ref[GROUPS + g] = high
             low_ref[GROUPS + g] = low
-        scatter_slots(GROUPS // 2, node_ref, elem_ref, high_ref, low_ref, left_ref, sum_ref)
+        scatter_slots(GROUPS, node_ref, hot_ref, high_ref, low_ref, left_ref, sum_ref)
 
     forces(0, value_ref)
 
@@ -443,9 +496,10 @@
     pull = pulls(0, box_now)
     box_next = 2.0 * box_now - box_before + STEP_SCALE * pull / mass
     reactions(0)
-    advance(j, value_ref, old_ref, force_ref, sum_ref, node_mass_ref, modes_ref, next_ref)
-
-    fill_table(next_ref, node_ref, elem_ref, table_ref)
+    advance(j, value_ref, old_ref, force_ref, sum_ref, node_mass_ref, modes_ref, next_ref,
+            pieces_ref)
+
+    fill_table(next_ref, pieces_ref, hot_ref, node_ref, elem_ref, table_ref)
 
     def sample_peer(o):
         sample_block(1, lax.rem(j + BOX - o, BOX))
@@ -495,6 +549,24 @@
             copy.wait_send()
     result.wait()
     box_result.wait()
+
+
+PIECES = 8
+
+
+def hand_over_kernel(final_ref, box_ref, out_ref, box_out_ref, sem):
+    rows = NODES * COLS // PIECES
+    copies = [
+        pltpu.make_async_copy(
+            final_ref.at[k * rows : (k + 1) * rows], out_ref.at[k * rows : (k + 1) * rows],
+            sem.at[k])
+        for k in range(PIECES)
+    ]
+    copies.append(pltpu.make_async_copy(box_ref, box_out_ref, sem.at[PIECES]))
+    for copy in copies:
+        copy.start()
+    for copy in copies:
+        copy.wait()
 
 
 def per_device(
@@ -513,7 +585,9 @@
         radial_modulus, shear_modulus, node_mass, element_modes.reshape(1, ELEMS),
     ]
     vmem = pltpu.VMEM
-    scratch = [vmem(x.shape, x.dtype) for x in args] + [
+    scratch = [vmem(x.shape, x.dtype) for x in args]
+    scratch[VALUES] = vmem((PADDED, ELEMS), F32)
+    scratch += [
         vmem((8, 8, 128), F32),
         vmem((8, 128), I32),
         vmem((8, 8, 128), F32),
@@ -525,11 +599,11 @@
         vmem((ROWS, COLS, 128), F32),
         vmem((GROUPS, COLS, 128), F32),
         vmem((flat, ELEMS), F32),
-        vmem((flat, ELEMS), F32),
+        vmem((PADDED, ELEMS), F32),
         vmem((flat, ELEMS), F32),
         vmem((ALL_GROUPS, COLS, 128), BF16),
         vmem((ALL_GROUPS, COLS, 128), BF16),
-        vmem((PAIRS * COLS, 512), BF16),
+        vmem((PAIRS * COLS, 1024), BF16),
         vmem((PAIRS * COLS, 256), F32),
         vmem((2, 4, COLS, 128), F32),
         vmem((2, 4, COLS, 128), F32),
@@ -540,6 +614,9 @@
         vmem((8, 8, 128), F32),
         vmem((MER, 8, 128), F32),
         vmem((8, 128), F32),
+        vmem((PAIRS * COLS, 512), BF16),
+        vmem((ALL_GROUPS, 256, 128), BF16),
+        vmem((128, 128), F32),
     ]
     dma = pltpu.SemaphoreType.DMA
     scratch += [dma((INPUTS,))] + [dma((MER,))] * 2 + [dma((BOX,))] * 2 + [dma((2, 2))] * 2
@@ -555,6 +632,14 @@
             vmem_limit_bytes=56 << 20, collective_id=0, has_side_effects=True),
         name="coupled_steps",
     )(*args)
+    final, box_out = pl.pallas_call(
+        hand_over_kernel,
+        out_shape=[jax.ShapeDtypeStruct((flat, ELEMS), F32), jax.ShapeDtypeStruct((8, 128), F32)],
+        in_specs=[any_space] * 2,
+        out_specs=[any_space] * 2,
+        scratch_shapes=[dma((PIECES + 1,))],
+        name="hand_over",
+    )(final, box_out)
     return final.reshape(NODES, COLS, ELEMS), box_out.reshape(1024)
 
 

time: 73.1 us -> 77.5 us (1.060)
  Pallas kernels: 69.5 us -> 76.7 us
  local copies, waits for them, and re-layouts: 2.72 us -> 0 us
    pallas_call x0 -> x1, Pallas kernels: none -> 26.1 us  [per_device(): pl.pallas_call(hand_over_kernel, out_shape=[jax.ShapeDtypeStruct((flat, E...]
    pallas_call x1, Pallas kernels: 69.5 us -> 50.6 us  [per_device(): pl.pallas_call(whole_kernel, out_shape=[jax.ShapeDtypeStruct((flat, ELEMS...]
    unnamed x4 -> x0, local copies, waits for them, and re-layouts: 2.72 us -> none
where the time goes in v2:
time: 77.5 us; the launch traced here: 77.3 us
  Pallas kernels  76.7 us (99%)
    pallas_call x1, Pallas kernels, per_device(): pl.pallas_call(whole_kernel, out_shape=[jax.ShapeDtypeStruct((flat, ELEMS...  50.6 us
    pallas_call x1, Pallas kernels, per_device(): pl.pallas_call(hand_over_kernel, out_shape=[jax.ShapeDtypeStruct((flat, E...  26.1 us

profile of v2, /device:TPU:1, one launch (start us, length us, event | category | flops | bytes accessed | tf_op | source)
XLA Modules:
  0.0 77.3 jit_solution(9183006941366262131)
XLA Ops:
  0.6 50.6 %coupled_steps.1 = (f32[1600,128]{1,0:T(8,128)}, f32[8,128]{1,0:T(8,128)}) custom-call(f32[8,128]{1,0:T(8,128)} %bitcast.20, s32[8,128]{1,0:T(8,128)} %bitcast.21, f32[8,128]{1,0:T(8,128)} %bitcast.22, f32[8,128]{1,0:T(8,128)} %bitcast.23, f32[8,128]{1,0:T(8,128)} %bitcast.24, f32[8,128]{1,0:T(8,128)} %bitcast.25, f32[8,128]{1,0:T(8,128)} %bitcast.26, ...), custom_call_target="tpu_custom_call" | custom-call | tf_op jit(solution)/shard_map/coupled_steps/pallas_call | solution.py:625
  51.2 26.1 %hand_over.1 = (f32[1600,128]{1,0:T(8,128)}, f32[8,128]{1,0:T(8,128)}) custom-call(f32[1600,128]{1,0:T(8,128)} %get-tuple-element.6.final_ref, f32[8,128]{1,0:T(8,128)} %get-tuple-element.7.box_ref), custom_call_target="tpu_custom_call" | custom-call | tf_op jit(solution)/shard_map/hand_over/pallas_call | solution.py:635

commit v3 on v2

--- a/solution.py
+++ b/solution.py
@@ -14,8 +14,9 @@
 MODES = 256
 NODES, COLS, ELEMS = 25, 64, 128
 PAIRS = 13
-GROUPS = 32
-ALL_GROUPS = 36
+GROUPS = 16
+ALL_GROUPS = 20
+CHUNKS = 32
 ROWS = 64
 STEP_SCALE = 0.25
 
@@ -100,35 +101,67 @@
         send_ref[m] = sorted_fields[:, m * 128 : (m + 1) * 128]
 
 
-def slot_table(rows, target, edges, node_ref, elem_ref):
+def pick_rows(shape, source):
+    return hot(iota(shape, 1) == source(iota(shape, 0)))
+
+
+def row_table(rows, target, edges, node_ref, elem_ref, start_ref, count_ref, meta_ref, shift_ref):
     tri = before_lane()
     reader = (target & (BOX - 1)) * MER + (target >> 3)
-    node1 = ((rows >> 7) + 1).astype(F32)
+    node = (rows >> 7).astype(F32)
     elem = (rows & 127).astype(F32)
-    count = jnp.zeros((128, 1), F32)
-    table = jnp.zeros((64, 128), F32)
+    readers = iota((128, 128), 0)
+    seen = jnp.zeros((128, 128), F32)
+    for r in range(16):
+        seen = seen + jnp.where(readers == reader[r : r + 1, :], 1.0, 0.0)
+    count = jnp.sum(seen, axis=1, keepdims=True)
+    wide = jnp.broadcast_to(count, (128, 128)).astype(BF16)
+    below = hot(iota((128, 128), 1) < iota((128, 128), 0))
+    start = dot(below, wide)
+    base = start
+    table = jnp.zeros((2 * GROUPS, 128), F32)
     for r in range(16):
         mine = reader[r : r + 1, :]
-        member = jnp.where(iota((128, 128), 0) == mine, 1.0, 0.0)
-        rank = dot(member.astype(BF16), tri) + count
+        member = jnp.where(readers == mine, 1.0, 0.0)
+        rank = dot(member.astype(BF16), tri) + base
         place = jnp.sum(member * rank, axis=0, keepdims=True).astype(I32)
-        count = count + jnp.sum(member, axis=1, keepdims=True)
-        lane = (mine & 3) * 32 + place
-        group = iota((GROUPS, 128), 0) == (mine >> 2)
+        base = base + jnp.sum(member, axis=1, keepdims=True)
+        group = iota((GROUPS, 128), 0) == (place >> 7)
         values = jnp.concatenate(
             [
-                jnp.where(group, jnp.broadcast_to(node1[r : r + 1, :], (GROUPS, 128)), 0.0),
+                jnp.where(group, jnp.broadcast_to(node[r : r + 1, :], (GROUPS, 128)), 0.0),
                 jnp.where(group, jnp.broadcast_to(elem[r : r + 1, :], (GROUPS, 128)), 0.0),
             ],
             axis=0,
         ).astype(BF16)
-        table = table + dot_nt(values, hot(iota((128, 128), 0) == lane))
-    node_ref[0:GROUPS, :] = table[0:GROUPS].astype(I32) - 1
+        table = table + dot_nt(values, hot(readers == (place & 127)))
+    node_ref[0:GROUPS, :] = table[0:GROUPS].astype(I32)
     elem_ref[0:GROUPS, :] = table[GROUPS : 2 * GROUPS].astype(I32)
     for k, edge in enumerate(edges):
         node_ref[GROUPS + 2 * k : GROUPS + 2 * k + 2, :] = edge >> 7
         elem_ref[GROUPS + 2 * k : GROUPS + 2 * k + 2, :] = edge & 127
 
+    high = jnp.floor(start * (1.0 / 16.0))
+    parts = [high.astype(BF16), (start - 16.0 * high).astype(BF16)]
+    same_half = (iota((128, 128), 0) & 1) == (iota((128, 128), 1) >> 6)
+
+    def halved(x):
+        return jnp.where(same_half, x.astype(F32), 0.0).astype(BF16)
+
+    def joined(left, right):
+        return (16.0 * dot(left, right[0]) + dot(left, right[1])).astype(I32)
+
+    own = hot((iota((ROWS, 128), 1) >> 1) == iota((ROWS, 128), 0))
+    first = joined(pick_rows((ROWS, 128), lambda row: (row >> 1) * 4), parts) >> 7
+    start_ref[...] = joined(own, [halved(part) for part in parts]) - 128 * first
+    count_ref[...] = dot(own, halved(wide)).astype(I32)
+    group = joined(pick_rows((CHUNKS, 128), lambda chunk: chunk * 4), parts) >> 7
+    after = joined(pick_rows((CHUNKS, 128), lambda chunk: (chunk + 1) * 4), parts) >> 7
+    shift_ref[...] = after - group
+    meta_ref[0:CHUNKS, :] = group
+    last = jnp.sum(jnp.where(group <= iota((CHUNKS, 128), 1), 1, 0), axis=0, keepdims=True) - 1
+    meta_ref[CHUNKS : CHUNKS + 8, :] = jnp.broadcast_to(last, (8, 128))
+
 
 def halves(even, odd, half):
     low = jnp.where(half == 0, even, pltpu.roll(even, 64, 1))
@@ -136,7 +169,7 @@
     return jnp.where(iota((8, 128), 1) < 64, low, high)
 
 
-def harmonics(j, angles, block, harmonic_ref):
+def harmonics(j, angles, filled, block, harmonic_ref):
     sub = iota((8, 128), 0).astype(F32)
     first = (lax.rem(j, 4) * 64).astype(F32)
     is_sine = j >= 4
@@ -144,8 +177,9 @@
         angle = jnp.broadcast_to(angles[r : r + 1, :], (8, 128))
         base_sin, base_cos = sincos(angle * (sub + first))
         step_sin, step_cos = sincos(angle * (sub * 8.0))
-        a = jnp.where(is_sine, base_sin, base_cos)
-        b = jnp.where(is_sine, -base_cos, base_sin)
+        keep = jnp.broadcast_to(filled[r : r + 1, :], (8, 128)) > 0
+        a = jnp.where(keep, jnp.where(is_sine, base_sin, base_cos), 0.0)
+        b = jnp.where(keep, jnp.where(is_sine, -base_cos, base_sin), 0.0)
         for t in range(8):
             harmonic_ref[block * 8 + r, t * 8 : (t + 1) * 8, :] = (
                 a * step_cos[t : t + 1, :] - b * step_sin[t : t + 1, :]
@@ -207,19 +241,23 @@
     lax.fori_loop(0, GROUPS // (MATRIX_GROUPS + LANE_GROUPS), body, 0)
 
 
-def node_lane(place, odd):
-    return place + (iota((1, 128), 1) >> 6) * 32 + odd * 64
-
-
-def sample_nodes(table_ref, places, block, harmonic_ref):
+def sample_nodes(table_ref, local_ref, meta_ref, block, harmonic_ref):
     rows = []
     for r in range(8):
-        index = jnp.broadcast_to(node_lane(places[r : r + 1, :], r % 2), (8, 128))
-        group = block * 4 + r // 2
+        row = block * 8 + r
+        group = lax.clamp(0, meta_ref[block * 4 + r // 2, 0], GROUPS)
+        local = jnp.broadcast_to(local_ref[pl.ds(row, 1), :], (8, 128))
+        index = local & 127
+        second = local > 127
         acc = jnp.zeros((8, 128), F32)
         for c in range(8):
-            taken = take_lanes(table_ref[group, c * 8 : (c + 1) * 8, :], index)
-            acc = acc + taken * harmonic_ref[block * 8 + r, c * 8 : (c + 1) * 8, :]
+            columns = slice(c * 8, (c + 1) * 8)
+            taken = jnp.where(
+                second,
+                take_lanes(table_ref[group + 1, columns, :], index),
+                take_lanes(table_ref[group, columns, :], index),
+            )
+            acc = acc + taken * harmonic_ref[row, columns, :]
         rows.append(jnp.sum(acc, axis=0, keepdims=True))
     return jnp.concatenate(rows, axis=0)
 
@@ -270,28 +308,38 @@
     lax.fori_loop(0, 4, body, 0)
 
 
-def slot_reactions(drives, places, block, harmonic_ref, high_ref, low_ref):
+def row_reactions(drives, block, carry, local_ref, shift_ref, harmonic_ref, high_ref, low_ref):
     for k in range(4):
+        chunk = block * 4 + k
         pieces, hots = [], []
         for odd in range(2):
             r = 2 * k + odd
-            x = harmonic_ref[block * 8 + r] * drives[r : r + 1, :]
-            pieces.append(split2(x))
-            lane = node_lane(places[r : r + 1, :], odd)
-            hots.append(hot(iota((128, 128), 0) == lane))
-        left = jnp.concatenate([pieces[0][0], pieces[1][0], pieces[0][1], pieces[1][1]], axis=1)
-        right = jnp.concatenate(hots + hots, axis=1)
-        high, low = split2(dot_nt(left, right))
-        high_ref[block * 4 + k] = high
-        low_ref[block * 4 + k] = low
-
-
-def scatter_slots(first, node_ref, hot_ref, high_ref, low_ref, left_ref, sum_ref):
+            pieces.append(split2(harmonic_ref[block * 8 + r] * drives[r : r + 1, :]))
+            hots.append(hot(iota((256, 128), 0) == local_ref[pl.ds(block * 8 + r, 1), :]))
+        left = jnp.concatenate(
+            [
+                jnp.concatenate([pieces[0][p], pieces[1][p]], axis=1) for p in range(2)
+            ],
+            axis=0,
+        )
+        out = dot_nt(left, jnp.concatenate(hots, axis=1))
+        out = out[0:COLS] + out[COLS : 2 * COLS]
+        here = carry[0] + out[:, 0:128]
+        there = carry[1] + out[:, 128:256]
+        high, low = split2(here)
+        high_ref[chunk] = high
+        low_ref[chunk] = low
+        moved = jnp.broadcast_to(shift_ref[pl.ds(chunk, 1), :], (COLS, 128)) > 0
+        carry = (jnp.where(moved, there, here), jnp.where(moved, 0.0, there))
+    return carry
+
+
+def scatter_rows(sources, first, node_ref, hot_ref, high_ref, low_ref, left_ref, sum_ref):
     rights = []
     for h in range(4):
         pair = node_ref[pl.ds(first + h, 1), :] >> 1
-        high = high_ref[first + h]
-        low = low_ref[first + h]
+        high = high_ref[sources[h]]
+        low = low_ref[sources[h]]
         for a in range(PAIRS):
             mask = jnp.broadcast_to(hot(pair == a), (COLS, 128))
             rows = slice(a * 64, (a + 1) * 64)
@@ -329,7 +377,8 @@
         fields, dest_ref, send_ref, node_ref, elem_ref, received, share, shared, harmonic_ref,
         table_ref, force_ref, next_ref, last_ref, high_ref, low_ref, left_ref, sum_ref,
         edge_ref, edges, partial, sums, drive, drives, ways, returned, box_last,
-        pieces_ref, hot_ref, square_ref,
+        pieces_ref, hot_ref, square_ref, start_ref, count_ref, meta_ref, shift_ref, local_ref,
+        meta_smem, meta_sem,
         load_sem, send_sem, recv_sem, share_send, share_recv, edge_send, edge_recv,
         sum_send, sum_recv, drive_send, drive_recv, way_send, way_recv, out_sem,
     ) = refs[2 * INPUTS + 2 :]
@@ -409,7 +458,10 @@
     received[i] = send_ref[lax.div(i, 2)]
     for load in loads[7:]:
         load.wait()
-    slot_table(rows_ref[...], target_ref[...], (lower_ref[...], upper_ref[...]), node_ref, elem_ref)
+    row_table(rows_ref[...], target_ref[...], (lower_ref[...], upper_ref[...]), node_ref, elem_ref,
+              start_ref, count_ref, meta_ref, shift_ref)
+    meta = pltpu.make_async_copy(meta_ref, meta_smem, meta_sem.at[0])
+    meta.start()
     slot_hots(node_ref, elem_ref, hot_ref)
     square_ref[...] = jnp.zeros_like(square_ref)
     square_ref[0:NODES, 0:NODES] = deriv_ref[...]
@@ -420,7 +472,8 @@
     for lane in (128, 384):
         pieces_ref[(PAIRS - 1) * COLS : PAIRS * COLS, lane : lane + 128] = jnp.zeros(
             (COLS, 128), BF16)
-    fill_table(value_ref, pieces_ref, hot_ref, node_ref, elem_ref, table_ref)
+    table_ref[GROUPS : GROUPS + 2] = jnp.zeros((2, COLS, 128), F32)
+    meta.wait()
 
     repeat(1, MER, lambda o: to_part(o).wait_recv())
     half = lax.rem(i, 2)
@@ -442,8 +495,7 @@
             copy.start()
 
     def sample_block(step, block):
-        partial[step, block] = sample_nodes(
-            table_ref, shared[block, 1].astype(I32), block, harmonic_ref)
+        partial[step, block] = sample_nodes(table_ref, local_ref, meta_smem, block, harmonic_ref)
 
     def pulls(step, now):
         sample = partial[step, j]
@@ -456,33 +508,46 @@
         drives[step, j] = drive[step]
         return pull
 
-    def react(step, block):
-        slot_reactions(drives[step, block], shared[block, 1].astype(I32), block,
-                       harmonic_ref, high_ref, low_ref)
-        scatter_slots(block * 4, node_ref, hot_ref, high_ref, low_ref, left_ref, sum_ref)
-
     def reactions(step):
         sum_ref[...] = jnp.zeros_like(sum_ref)
-        react(step, j)
-
-        def work(o):
-            to_drive(step, o).wait_recv()
-            react(step, lax.rem(j + BOX - o, BOX))
-
-        repeat(1, BOX, work)
+
+        def work(block, carry):
+            @pl.when(block != j)
+            def _():
+                to_drive(step, lax.rem(j + BOX - block, BOX)).wait_recv()
+
+            return row_reactions(drives[step, block], block, carry, local_ref, shift_ref,
+                                 harmonic_ref, high_ref, low_ref)
+
+        nothing = jnp.zeros((COLS, 128), F32)
+        lax.fori_loop(0, BOX, work, (nothing, nothing))
+
+        def scatter(t, carry):
+            sources = [
+                lax.clamp(0, meta_smem[CHUNKS, t * 4 + h], CHUNKS - 1) for h in range(4)
+            ]
+            scatter_rows(sources, t * 4, node_ref, hot_ref, high_ref, low_ref, left_ref, sum_ref)
+            return carry
+
+        lax.fori_loop(0, GROUPS // 4, scatter, 0)
         for copy in to_edges(step):
             copy.wait_recv()
         for g in range(4):
             ghost = (i == 0) if g < 2 else (i == MER - 1)
             high, low = split2(jnp.where(ghost, 0.0, edges[step, g]))
-            high_ref[GROUPS + g] = high
-            low_ref[GROUPS + g] = low
-        scatter_slots(GROUPS, node_ref, hot_ref, high_ref, low_ref, left_ref, sum_ref)
-
-    forces(0, value_ref)
+            high_ref[CHUNKS + g] = high
+            low_ref[CHUNKS + g] = low
+        scatter_rows([CHUNKS + h for h in range(4)], GROUPS, node_ref, hot_ref, high_ref,
+                     low_ref, left_ref, sum_ref)
+
+    fill_table(value_ref, pieces_ref, hot_ref, node_ref, elem_ref, table_ref)
 
     def enter(block):
-        harmonics(j, shared[block, 0], block, harmonic_ref)
+        rows = pl.ds(pl.multiple_of(block * 8, 8), 8)
+        places = shared[block, 1].astype(I32)
+        filled = jnp.where(places < count_ref[rows, :], 1, 0)
+        local_ref[rows, :] = jnp.where(filled > 0, start_ref[rows, :] + places, 0)
+        harmonics(j, shared[block, 0], filled, block, harmonic_ref)
         sample_block(0, block)
 
     enter(j)
@@ -494,6 +559,7 @@
 
     repeat(1, BOX, enter_peer)
     pull = pulls(0, box_now)
+    forces(0, value_ref)
     box_next = 2.0 * box_now - box_before + STEP_SCALE * pull / mass
     reactions(0)
     advance(j, value_ref, old_ref, force_ref, sum_ref, node_mass_ref, modes_ref, next_ref,
@@ -507,13 +573,13 @@
 
     repeat(1, BOX, sample_peer)
     sample_block(1, j)
-    forces(1, next_ref)
     pull = pulls(1, box_next)
     box_after = 2.0 * box_next - box_now + STEP_SCALE * pull / mass
     for m in range(8):
         ways[m] = jnp.broadcast_to(box_after[m : m + 1, :], (8, 128))
     repeat(1, MER, lambda o: to_back(o).start())
     returned[i] = ways[lax.div(i, 2)]
+    forces(1, next_ref)
     reactions(1)
     advance(j, next_ref, value_ref, force_ref, sum_ref, node_mass_ref, modes_ref, last_ref)
     result = pltpu.make_async_copy(last_ref, out_ref, out_sem.at[0])
@@ -551,22 +617,25 @@
     box_result.wait()
 
 
-PIECES = 8
-
-
-def hand_over_kernel(final_ref, box_ref, out_ref, box_out_ref, sem):
-    rows = NODES * COLS // PIECES
+def hand_over_kernel(final_ref, box_ref, out_ref, box_out_ref, final, box, sem):
+    half = NODES * COLS // 2
+    parts = [
+        (final_ref.at[k * half : (k + 1) * half], final.at[k * half : (k + 1) * half],
+         out_ref.at[k * half : (k + 1) * half])
+        for k in range(2)
+    ] + [(box_ref, box, box_out_ref)]
     copies = [
-        pltpu.make_async_copy(
-            final_ref.at[k * rows : (k + 1) * rows], out_ref.at[k * rows : (k + 1) * rows],
-            sem.at[k])
-        for k in range(PIECES)
+        (pltpu.make_async_copy(source, middle, sem.at[0, k]),
+         pltpu.make_async_copy(middle, target, sem.at[1, k]))
+        for k, (source, middle, target) in enumerate(parts)
     ]
-    copies.append(pltpu.make_async_copy(box_ref, box_out_ref, sem.at[PIECES]))
-    for copy in copies:
-        copy.start()
-    for copy in copies:
-        copy.wait()
+    for first, second in copies:
+        first.start()
+    for first, second in copies:
+        first.wait()
+        second.start()
+    for first, second in copies:
+        second.wait()
 
 
 def per_device(
@@ -597,12 +666,12 @@
         vmem((2, 8, 128), F32),
         vmem((BOX, 2, 8, 128), F32),
         vmem((ROWS, COLS, 128), F32),
-        vmem((GROUPS, COLS, 128), F32),
+        vmem((GROUPS + 2, COLS, 128), F32),
         vmem((flat, ELEMS), F32),
         vmem((PADDED, ELEMS), F32),
         vmem((flat, ELEMS), F32),
-        vmem((ALL_GROUPS, COLS, 128), BF16),
-        vmem((ALL_GROUPS, COLS, 128), BF16),
+        vmem((CHUNKS + 4, COLS, 128), BF16),
+        vmem((CHUNKS + 4, COLS, 128), BF16),
         vmem((PAIRS * COLS, 1024), BF16),
         vmem((PAIRS * COLS, 256), F32),
         vmem((2, 4, COLS, 128), F32),
@@ -617,6 +686,13 @@
         vmem((PAIRS * COLS, 512), BF16),
         vmem((ALL_GROUPS, 256, 128), BF16),
         vmem((128, 128), F32),
+        vmem((ROWS, 128), I32),
+        vmem((ROWS, 128), I32),
+        vmem((CHUNKS + 8, 128), I32),
+        vmem((CHUNKS, 128), I32),
+        vmem((ROWS, 128), I32),
+        pltpu.SMEM((CHUNKS + 8, 128), I32),
+        pltpu.SemaphoreType.DMA((1,)),
     ]
     dma = pltpu.SemaphoreType.DMA
     scratch += [dma((INPUTS,))] + [dma((MER,))] * 2 + [dma((BOX,))] * 2 + [dma((2, 2))] * 2
@@ -637,7 +713,8 @@
         out_shape=[jax.ShapeDtypeStruct((flat, ELEMS), F32), jax.ShapeDtypeStruct((8, 128), F32)],
         in_specs=[any_space] * 2,
         out_specs=[any_space] * 2,
-        scratch_shapes=[dma((PIECES + 1,))],
+        scratch_shapes=[vmem((flat, ELEMS), F32), vmem((8, 128), F32), dma((2, 3))],
+        compiler_params=pltpu.CompilerParams(vmem_limit_bytes=60 << 20),
         name="hand_over",
     )(final, box_out)
     return final.reshape(NODES, COLS, ELEMS), box_out.reshape(1024)

time: 77.5 us -> 51.8 us (0.67)
  Pallas kernels: 76.7 us -> 51 us
    pallas_call x1, Pallas kernels: 26.1 us -> 1.94 us  [per_device(): pl.pallas_call(hand_over_kernel, out_shape=[jax.ShapeDtypeStruct((flat, E...]
    pallas_call x1, Pallas kernels: 50.6 us -> 49.1 us  [per_device(): pl.pallas_call(whole_kernel, out_shape=[jax.ShapeDtypeStruct((flat, ELEMS...]
where the time goes in v3:
time: 51.8 us; the launch traced here: 51.7 us
  Pallas kernels  51 us (98%)
  between operations  0.65 us (1%)
    pallas_call x1, Pallas kernels, per_device(): pl.pallas_call(whole_kernel, out_shape=[jax.ShapeDtypeStruct((flat, ELEMS...  49.1 us
    pallas_call x1, Pallas kernels, per_device(): pl.pallas_call(hand_over_kernel, out_shape=[jax.ShapeDtypeStruct((flat, E...  1.94 us

profile of v3, /device:TPU:1, one launch (start us, length us, event | category | flops | bytes accessed | tf_op | source)
XLA Modules:
  0.0 51.7 jit_solution(1286063010232845598)
XLA Ops:
  0.6 49.1 %coupled_steps.1 = (f32[1600,128]{1,0:T(8,128)}, f32[8,128]{1,0:T(8,128)}) custom-call(f32[8,128]{1,0:T(8,128)} %bitcast.20, s32[8,128]{1,0:T(8,128)} %bitcast.21, f32[8,128]{1,0:T(8,128)} %bitcast.22, f32[8,128]{1,0:T(8,128)} %bitcast.23, f32[8,128]{1,0:T(8,128)} %bitcast.24, f32[8,128]{1,0:T(8,128)} %bitcast.25, f32[8,128]{1,0:T(8,128)} %bitcast.26, ...), custom_call_target="tpu_custom_call" | custom-call | tf_op jit(solution)/shard_map/coupled_steps/pallas_call | solution.py:701
  49.7 1.9 %hand_over.1 = (f32[1600,128]{1,0:T(8,128)}, f32[8,128]{1,0:T(8,128)}) custom-call(f32[1600,128]{1,0:T(8,128)} %get-tuple-element.6.final_ref, f32[8,128]{1,0:T(8,128)} %get-tuple-element.7.box_ref), custom_call_target="tpu_custom_call" | custom-call | tf_op jit(solution)/shard_map/hand_over/pallas_call | solution.py:711

commit v4 on v3

--- a/solution.py
+++ b/solution.py
@@ -103,6 +103,14 @@
 
 def pick_rows(shape, source):
     return hot(iota(shape, 1) == source(iota(shape, 0)))
+
+
+def order_hots(dest_ref, order_ref):
+    def body(r, carry):
+        order_ref[r] = hot(iota((1024, 128), 0) == dest_ref[pl.ds(r, 1), :])
+        return carry
+
+    lax.fori_loop(0, 8, body, 0)
 
 
 def row_table(rows, target, edges, node_ref, elem_ref, start_ref, count_ref, meta_ref, shift_ref):
@@ -212,33 +220,30 @@
 def slot_hots(node_ref, elem_ref, hot_ref):
     def body(g, carry):
         lane = (node_ref[pl.ds(g, 1), :] & 1) * 128 + elem_ref[pl.ds(g, 1), :]
-        hot_ref[g] = hot(iota((256, 128), 0) == lane)
+        hot_ref[:, pl.ds(pl.multiple_of(g * 128, 128), 128)] = hot(iota((256, 128), 0) == lane)
         return carry
 
     lax.fori_loop(0, ALL_GROUPS, body, 0)
 
 
 def fill_table(values_ref, pieces_ref, hot_ref, node_ref, elem_ref, table_ref):
-    def body(t, carry):
+    for t in range(GROUPS // (MATRIX_GROUPS + LANE_GROUPS)):
         first = t * (MATRIX_GROUPS + LANE_GROUPS)
-        right = jnp.concatenate([hot_ref[first + k] for k in range(MATRIX_GROUPS)], axis=1)
+        right = hot_ref[:, first * 128 : (first + MATRIX_GROUPS) * 128]
         out = dot(pieces_ref[...], jnp.concatenate([right, right], axis=0))
         for k in range(LANE_GROUPS):
             g = first + MATRIX_GROUPS + k
-            acc = gather_rows(values_ref, node_ref[pl.ds(g, 1), :], elem_ref[pl.ds(g, 1), :])
+            acc = gather_rows(values_ref, node_ref[g : g + 1, :], elem_ref[g : g + 1, :])
             for c in range(8):
                 table_ref[g, c * 8 : (c + 1) * 8, :] = acc[c]
         for k in range(MATRIX_GROUPS):
             g = first + k
-            pair = node_ref[pl.ds(g, 1), :] >> 1
+            pair = node_ref[g : g + 1, :] >> 1
             acc = jnp.zeros((COLS, 128), F32)
             for a in range(PAIRS):
                 acc = jnp.where(
                     pair == a, out[a * 64 : (a + 1) * 64, k * 128 : (k + 1) * 128], acc)
             table_ref[g] = acc
-        return carry
-
-    lax.fori_loop(0, GROUPS // (MATRIX_GROUPS + LANE_GROUPS), body, 0)
 
 
 def sample_nodes(table_ref, local_ref, meta_ref, block, harmonic_ref):
@@ -308,21 +313,30 @@
     lax.fori_loop(0, 4, body, 0)
 
 
-def row_reactions(drives, block, carry, local_ref, shift_ref, harmonic_ref, high_ref, low_ref):
+def chunk_hots(local_ref, near_ref):
+    def body(chunk, carry):
+        for odd in range(2):
+            near_ref[chunk, :, odd * 128 : (odd + 1) * 128] = hot(
+                iota((256, 128), 0) == local_ref[pl.ds(chunk * 2 + odd, 1), :])
+        return carry
+
+    lax.fori_loop(0, CHUNKS, body, 0)
+
+
+def row_reactions(drives, block, carry, near_ref, shift_ref, harmonic_ref, high_ref, low_ref):
     for k in range(4):
         chunk = block * 4 + k
-        pieces, hots = [], []
-        for odd in range(2):
-            r = 2 * k + odd
-            pieces.append(split2(harmonic_ref[block * 8 + r] * drives[r : r + 1, :]))
-            hots.append(hot(iota((256, 128), 0) == local_ref[pl.ds(block * 8 + r, 1), :]))
+        pieces = [
+            split2(harmonic_ref[chunk * 2 + odd] * drives[2 * k + odd : 2 * k + odd + 1, :])
+            for odd in range(2)
+        ]
         left = jnp.concatenate(
             [
                 jnp.concatenate([pieces[0][p], pieces[1][p]], axis=1) for p in range(2)
             ],
             axis=0,
         )
-        out = dot_nt(left, jnp.concatenate(hots, axis=1))
+        out = dot_nt(left, near_ref[chunk])
         out = out[0:COLS] + out[COLS : 2 * COLS]
         here = carry[0] + out[:, 0:128]
         there = carry[1] + out[:, 128:256]
@@ -334,19 +348,17 @@
     return carry
 
 
-def scatter_rows(sources, first, node_ref, hot_ref, high_ref, low_ref, left_ref, sum_ref):
-    rights = []
-    for h in range(4):
-        pair = node_ref[pl.ds(first + h, 1), :] >> 1
-        high = high_ref[sources[h]]
-        low = low_ref[sources[h]]
-        for a in range(PAIRS):
-            mask = jnp.broadcast_to(hot(pair == a), (COLS, 128))
-            rows = slice(a * 64, (a + 1) * 64)
-            left_ref[rows, h * 128 : (h + 1) * 128] = high * mask
-            left_ref[rows, 512 + h * 128 : 640 + h * 128] = low * mask
-        rights.append(hot_ref[first + h])
-    sum_ref[...] += dot_nt(left_ref[...], jnp.concatenate(rights + rights, axis=1))
+def place_rows(high, low, node, lanes, left_ref):
+    pair = node >> 1
+    for a in range(PAIRS):
+        mask = jnp.broadcast_to(hot(pair == a), (COLS, 128))
+        left_ref[a * 64 : (a + 1) * 64, lanes] = high * mask
+        left_ref[(PAIRS + a) * 64 : (PAIRS + a + 1) * 64, lanes] = low * mask
+
+
+def scatter_rows(hot_ref, left_ref, sum_ref):
+    out = dot_nt(left_ref[...], hot_ref[...])
+    sum_ref[...] = out[0 : PAIRS * COLS] + out[PAIRS * COLS : 2 * PAIRS * COLS]
 
 
 def advance(j, now_ref, before_ref, force_ref, sum_ref, mass_ref, modes_ref, next_ref,
@@ -375,12 +387,12 @@
     vmem = refs[INPUTS + 2 : 2 * INPUTS + 2]
     (
         fields, dest_ref, send_ref, node_ref, elem_ref, received, share, shared, harmonic_ref,
-        table_ref, force_ref, next_ref, last_ref, high_ref, low_ref, left_ref, sum_ref,
-        edge_ref, edges, partial, sums, drive, drives, ways, returned, box_last,
+        table_ref, force_ref, next_ref, high_ref, low_ref, left_ref, sum_ref,
+        edge_ref, edges, partial, sums, drive, drives, ways, returned,
         pieces_ref, hot_ref, square_ref, start_ref, count_ref, meta_ref, shift_ref, local_ref,
-        meta_smem, meta_sem,
+        meta_smem, meta_sem, near_ref, order_ref,
         load_sem, send_sem, recv_sem, share_send, share_recv, edge_send, edge_recv,
-        sum_send, sum_recv, drive_send, drive_recv, way_send, way_recv, out_sem,
+        sum_send, sum_recv, drive_send, drive_recv, way_send, way_recv,
     ) = refs[2 * INPUTS + 2 :]
     (
         angle_ref, slot_ref, spring_ref, mass_ref, weight_ref, now_ref, before_ref,
@@ -398,7 +410,7 @@
         return vmem[k]
 
     loads = [pltpu.make_async_copy(hbm[k], landing(k), load_sem.at[k]) for k in range(INPUTS)]
-    for load in loads:
+    for load in loads[:7]:
         load.start()
     barrier = pltpu.get_barrier_semaphore()
     for o in range(1, MER):
@@ -407,6 +419,9 @@
     for o in range(1, BOX):
         pl.semaphore_signal(
             barrier, inc=1, device_id=(i, lax.rem(j + o, BOX)), device_id_type=MESH)
+
+    for load in loads[7:]:
+        load.start()
 
     def way(source, target, send, recv, device):
         return pltpu.make_async_remote_copy(
@@ -508,37 +523,37 @@
         drives[step, j] = drive[step]
         return pull
 
-    def reactions(step):
-        sum_ref[...] = jnp.zeros_like(sum_ref)
-
+    def reactions(step, between):
         def work(block, carry):
             @pl.when(block != j)
             def _():
                 to_drive(step, lax.rem(j + BOX - block, BOX)).wait_recv()
 
-            return row_reactions(drives[step, block], block, carry, local_ref, shift_ref,
+            return row_reactions(drives[step, block], block, carry, near_ref, shift_ref,
                                  harmonic_ref, high_ref, low_ref)
 
         nothing = jnp.zeros((COLS, 128), F32)
         lax.fori_loop(0, BOX, work, (nothing, nothing))
-
-        def scatter(t, carry):
-            sources = [
-                lax.clamp(0, meta_smem[CHUNKS, t * 4 + h], CHUNKS - 1) for h in range(4)
-            ]
-            scatter_rows(sources, t * 4, node_ref, hot_ref, high_ref, low_ref, left_ref, sum_ref)
+        between()
+
+        def place(t, carry):
+            for h in range(4):
+                g = t * 4 + h
+                source = lax.clamp(0, meta_smem[CHUNKS, g], CHUNKS - 1)
+                lanes = pl.ds(pl.multiple_of(t * 512, 512) + h * 128, 128)
+                place_rows(high_ref[source], low_ref[source], node_ref[pl.ds(g, 1), :], lanes,
+                           left_ref)
             return carry
 
-        lax.fori_loop(0, GROUPS // 4, scatter, 0)
+        lax.fori_loop(0, GROUPS // 4, place, 0)
         for copy in to_edges(step):
             copy.wait_recv()
         for g in range(4):
             ghost = (i == 0) if g < 2 else (i == MER - 1)
             high, low = split2(jnp.where(ghost, 0.0, edges[step, g]))
-            high_ref[CHUNKS + g] = high
-            low_ref[CHUNKS + g] = low
-        scatter_rows([CHUNKS + h for h in range(4)], GROUPS, node_ref, hot_ref, high_ref,
-                     low_ref, left_ref, sum_ref)
+            k = GROUPS + g
+            place_rows(high, low, node_ref[k : k + 1, :], slice(k * 128, (k + 1) * 128), left_ref)
+        scatter_rows(hot_ref, left_ref, sum_ref)
 
     fill_table(value_ref, pieces_ref, hot_ref, node_ref, elem_ref, table_ref)
 
@@ -558,10 +573,11 @@
         to_sum(0, o).start()
 
     repeat(1, BOX, enter_peer)
+    chunk_hots(local_ref, near_ref)
     pull = pulls(0, box_now)
     forces(0, value_ref)
     box_next = 2.0 * box_now - box_before + STEP_SCALE * pull / mass
-    reactions(0)
+    reactions(0, lambda: None)
     advance(j, value_ref, old_ref, force_ref, sum_ref, node_mass_ref, modes_ref, next_ref,
             pieces_ref)
 
@@ -573,17 +589,15 @@
 
     repeat(1, BOX, sample_peer)
     sample_block(1, j)
+    order_hots(dest_ref, order_ref)
     pull = pulls(1, box_next)
     box_after = 2.0 * box_next - box_now + STEP_SCALE * pull / mass
     for m in range(8):
         ways[m] = jnp.broadcast_to(box_after[m : m + 1, :], (8, 128))
-    repeat(1, MER, lambda o: to_back(o).start())
     returned[i] = ways[lax.div(i, 2)]
     forces(1, next_ref)
-    reactions(1)
-    advance(j, next_ref, value_ref, force_ref, sum_ref, node_mass_ref, modes_ref, last_ref)
-    result = pltpu.make_async_copy(last_ref, out_ref, out_sem.at[0])
-    result.start()
+    reactions(1, lambda: repeat(1, MER, lambda o: to_back(o).start()))
+    advance(j, next_ref, value_ref, force_ref, sum_ref, node_mass_ref, modes_ref, out_ref)
 
     repeat(1, MER, lambda o: to_back(o).wait_recv())
     even = jnp.concatenate([returned[2 * r, 0:1, :] for r in range(8)], axis=0)
@@ -592,10 +606,8 @@
     line = jnp.concatenate([box[m : m + 1, :] for m in range(8)], axis=1)
     pieces = jnp.concatenate([piece.astype(F32) for piece in split3(line)], axis=0).astype(BF16)
     for r in range(8):
-        out = dot(pieces, hot(iota((1024, 128), 0) == dest_ref[r : r + 1, :]))
-        box_last[r : r + 1, :] = out[0:1] + (out[1:2] + out[2:3])
-    box_result = pltpu.make_async_copy(box_last, box_out_ref, out_sem.at[1])
-    box_result.start()
+        out = dot(pieces, order_ref[r])
+        box_out_ref[r : r + 1, :] = out[0:1] + (out[1:2] + out[2:3])
 
     def sent(o):
         to_share(o).wait_send()
@@ -613,29 +625,17 @@
     for step in range(2):
         for copy in to_edges(step):
             copy.wait_send()
-    result.wait()
-    box_result.wait()
-
-
-def hand_over_kernel(final_ref, box_ref, out_ref, box_out_ref, final, box, sem):
-    half = NODES * COLS // 2
-    parts = [
-        (final_ref.at[k * half : (k + 1) * half], final.at[k * half : (k + 1) * half],
-         out_ref.at[k * half : (k + 1) * half])
-        for k in range(2)
-    ] + [(box_ref, box, box_out_ref)]
+
+
+def hand_over_kernel(final_ref, box_ref, out_ref, box_out_ref, sem):
     copies = [
-        (pltpu.make_async_copy(source, middle, sem.at[0, k]),
-         pltpu.make_async_copy(middle, target, sem.at[1, k]))
-        for k, (source, middle, target) in enumerate(parts)
+        pltpu.make_async_copy(final_ref, out_ref, sem.at[0]),
+        pltpu.make_async_copy(box_ref, box_out_ref, sem.at[1]),
     ]
-    for first, second in copies:
-        first.start()
-    for first, second in copies:
-        first.wait()
-        second.start()
-    for first, second in copies:
-        second.wait()
+    for copy in copies:
+        copy.start()
+    for copy in copies:
+        copy.wait()
 
 
 def per_device(
@@ -669,10 +669,9 @@
         vmem((GROUPS + 2, COLS, 128), F32),
         vmem((flat, ELEMS), F32),
         vmem((PADDED, ELEMS), F32),
-        vmem((flat, ELEMS), F32),
-        vmem((CHUNKS + 4, COLS, 128), BF16),
-        vmem((CHUNKS + 4, COLS, 128), BF16),
-        vmem((PAIRS * COLS, 1024), BF16),
+        vmem((CHUNKS, COLS, 128), BF16),
+        vmem((CHUNKS, COLS, 128), BF16),
+        vmem((2 * PAIRS * COLS, ALL_GROUPS * 128), BF16),
         vmem((PAIRS * COLS, 256), F32),
         vmem((2, 4, COLS, 128), F32),
         vmem((2, 4, COLS, 128), F32),
@@ -682,9 +681,8 @@
         vmem((2, BOX, 8, 128), F32),
         vmem((8, 8, 128), F32),
         vmem((MER, 8, 128), F32),
-        vmem((8, 128), F32),
         vmem((PAIRS * COLS, 512), BF16),
-        vmem((ALL_GROUPS, 256, 128), BF16),
+        vmem((256, ALL_GROUPS * 128), BF16),
         vmem((128, 128), F32),
         vmem((ROWS, 128), I32),
         vmem((ROWS, 128), I32),
@@ -693,28 +691,30 @@
         vmem((ROWS, 128), I32),
         pltpu.SMEM((CHUNKS + 8, 128), I32),
         pltpu.SemaphoreType.DMA((1,)),
+        vmem((CHUNKS, 256, 256), BF16),
+        vmem((8, 1024, 128), BF16),
     ]
     dma = pltpu.SemaphoreType.DMA
     scratch += [dma((INPUTS,))] + [dma((MER,))] * 2 + [dma((BOX,))] * 2 + [dma((2, 2))] * 2
-    scratch += [dma((2, BOX))] * 4 + [dma((MER,))] * 2 + [dma((2,))]
+    scratch += [dma((2, BOX))] * 4 + [dma((MER,))] * 2
     any_space = pl.BlockSpec(memory_space=pl.ANY)
     final, box_out = pl.pallas_call(
         whole_kernel,
         out_shape=[jax.ShapeDtypeStruct((flat, ELEMS), F32), jax.ShapeDtypeStruct((8, 128), F32)],
-        in_specs=[any_space] * INPUTS,
-        out_specs=[any_space] * 2,
+        in_specs=[pl.BlockSpec(memory_space=pltpu.HBM)] * INPUTS,
+        out_specs=[pl.BlockSpec(memory_space=pltpu.VMEM)] * 2,
         scratch_shapes=scratch,
         compiler_params=pltpu.CompilerParams(
-            vmem_limit_bytes=56 << 20, collective_id=0, has_side_effects=True),
+            vmem_limit_bytes=44 << 20, collective_id=0, has_side_effects=True),
         name="coupled_steps",
-    )(*args)
+    )(*[pltpu.with_memory_space_constraint(x, pltpu.HBM) for x in args])
     final, box_out = pl.pallas_call(
         hand_over_kernel,
         out_shape=[jax.ShapeDtypeStruct((flat, ELEMS), F32), jax.ShapeDtypeStruct((8, 128), F32)],
-        in_specs=[any_space] * 2,
+        in_specs=[pl.BlockSpec(memory_space=pltpu.VMEM)] * 2,
         out_specs=[any_space] * 2,
-        scratch_shapes=[vmem((flat, ELEMS), F32), vmem((8, 128), F32), dma((2, 3))],
-        compiler_params=pltpu.CompilerParams(vmem_limit_bytes=60 << 20),
+        scratch_shapes=[dma((2,))],
+        compiler_params=pltpu.CompilerParams(vmem_limit_bytes=4 << 20),
         name="hand_over",
     )(final, box_out)
     return final.reshape(NODES, COLS, ELEMS), box_out.reshape(1024)

time: 51.8 us -> 54.3 us (1.048)
  Pallas kernels: 51 us -> 53.5 us
    pallas_call x1, Pallas kernels: 49.1 us -> 52.6 us  [per_device(): pl.pallas_call(whole_kernel, out_shape=[jax.ShapeDtypeStruct((flat, ELEMS...]
    pallas_call x1, Pallas kernels: 1.94 us -> 0.91 us  [per_device(): pl.pallas_call(hand_over_kernel, out_shape=[jax.ShapeDtypeStruct((flat, E...]
where the time goes in v4:
time: 54.3 us; the launch traced here: 54.1 us
  Pallas kernels  53.5 us (99%)
  between operations  0.65 us (1%)
    pallas_call x1, Pallas kernels, per_device(): pl.pallas_call(whole_kernel, out_shape=[jax.ShapeDtypeStruct((flat, ELEMS...  52.6 us

profile of v4, /device:TPU:1, one launch (start us, length us, event | category | flops | bytes accessed | tf_op | source)
XLA Modules:
  0.0 54.1 jit_solution(17324157172353397137)
XLA Ops:
  0.6 52.6 %coupled_steps.1 = (f32[1600,128]{1,0:T(8,128)S(1)}, f32[8,128]{1,0:T(8,128)S(1)}) custom-call(f32[8,128]{1,0:T(8,128)} %bitcast.20, s32[8,128]{1,0:T(8,128)} %bitcast.21, f32[8,128]{1,0:T(8,128)} %bitcast.22, f32[8,128]{1,0:T(8,128)} %bitcast.23, f32[8,128]{1,0:T(8,128)} %bitcast.24, f32[8,128]{1,0:T(8,128)} %bitcast.25, f32[8,128]{1,0:T(8,128)} %bitcast.26, ...), custom_call_target="tpu_custom_call" | custom-call | tf_op jit(solution)/shard_map/coupled_steps/pallas_call | solution.py:701
  53.2 0.9 %hand_over.1 = (f32[1600,128]{1,0:T(8,128)}, f32[8,128]{1,0:T(8,128)}) custom-call(f32[1600,128]{1,0:T(8,128)S(1)} %get-tuple-element.6.final_ref, f32[8,128]{1,0:T(8,128)S(1)} %get-tuple-element.7.box_ref), custom_call_target="tpu_custom_call" | custom-call | tf_op jit(solution)/shard_map/hand_over/pallas_call | solution.py:711

commit v5 on v3

--- a/solution.py
+++ b/solution.py
@@ -267,7 +267,7 @@
     return jnp.concatenate([high, high, low], axis=1)
 
 
-def compute_force(j, values_ref, deriv_ref, radial_ref, shear_ref, force_ref):
+def compute_force(j, half, values_ref, deriv_ref, radial_ref, shear_ref, force_ref):
     deriv = deriv_ref[...]
     stack = small_stack(deriv[0:32, 0:32])
     stack_t = small_stack(deriv.T[0:32, 0:32])
@@ -293,7 +293,7 @@
             )
         return carry
 
-    lax.fori_loop(0, 4, body, 0)
+    lax.fori_loop(2 * half, 2 * half + 2, body, 0)
 
 
 def edge_forces(force_ref, node_ref, elem_ref, edge_ref):
@@ -352,13 +352,15 @@
 def advance(j, now_ref, before_ref, force_ref, sum_ref, mass_ref, modes_ref, next_ref,
             pieces_ref=None):
     order = lax.rem(j, 4) * 64 + iota((COLS, 128), 0)
-    live = jnp.where(order < modes_ref[...], STEP_SCALE, 0.0)
+    live = order < modes_ref[...]
+    scale = STEP_SCALE / mass_ref[...]
     for a in range(NODES):
         rows = slice(a * 64, (a + 1) * 64)
         pair = a // 2
         lanes = slice((a % 2) * 128, (a % 2) * 128 + 128)
         total = force_ref[rows, :] + sum_ref[pair * 64 : (pair + 1) * 64, lanes]
-        after = 2.0 * now_ref[rows, :] - before_ref[rows, :] + live * total / mass_ref[a : a + 1, :]
+        after = 2.0 * now_ref[rows, :] - before_ref[rows, :]
+        after = after + jnp.where(live, scale[a : a + 1, :], 0.0) * total
         next_ref[rows, :] = after
         if pieces_ref is not None:
             keep_pieces(after, a, pieces_ref)
@@ -398,7 +400,7 @@
         return vmem[k]
 
     loads = [pltpu.make_async_copy(hbm[k], landing(k), load_sem.at[k]) for k in range(INPUTS)]
-    for load in loads:
+    for load in loads[:7]:
         load.start()
     barrier = pltpu.get_barrier_semaphore()
     for o in range(1, MER):
@@ -407,6 +409,9 @@
     for o in range(1, BOX):
         pl.semaphore_signal(
             barrier, inc=1, device_id=(i, lax.rem(j + o, BOX)), device_id_type=MESH)
+
+    for load in loads[7:]:
+        load.start()
 
     def way(source, target, send, recv, device):
         return pltpu.make_async_remote_copy(
@@ -488,8 +493,11 @@
     shared[j] = share[...]
     spring, mass, weight, box_now, box_before = own[2:]
 
+    def first_forces(ref):
+        compute_force(j, 0, ref, square_ref, radial_ref, shear_ref, force_ref)
+
     def forces(step, ref):
-        compute_force(j, ref, square_ref, radial_ref, shear_ref, force_ref)
+        compute_force(j, 1, ref, square_ref, radial_ref, shear_ref, force_ref)
         edge_forces(force_ref, node_ref, elem_ref, edge_ref.at[step])
         for copy in to_edges(step):
             copy.start()
@@ -511,16 +519,19 @@
     def reactions(step):
         sum_ref[...] = jnp.zeros_like(sum_ref)
 
-        def work(block, carry):
-            @pl.when(block != j)
-            def _():
-                to_drive(step, lax.rem(j + BOX - block, BOX)).wait_recv()
-
-            return row_reactions(drives[step, block], block, carry, local_ref, shift_ref,
-                                 harmonic_ref, high_ref, low_ref)
+        def work(k, carry):
+            for block in (2 * k, 2 * k + 1):
+                @pl.when(block != j)
+                def _():
+                    to_drive(step, lax.rem(j + BOX - block, BOX)).wait_recv()
+
+            for block in (2 * k, 2 * k + 1):
+                carry = row_reactions(drives[step, block], block, carry, local_ref, shift_ref,
+                                      harmonic_ref, high_ref, low_ref)
+            return carry
 
         nothing = jnp.zeros((COLS, 128), F32)
-        lax.fori_loop(0, BOX, work, (nothing, nothing))
+        lax.fori_loop(0, BOX // 2, work, (nothing, nothing))
 
         def scatter(t, carry):
             sources = [
@@ -558,6 +569,7 @@
         to_sum(0, o).start()
 
     repeat(1, BOX, enter_peer)
+    first_forces(value_ref)
     pull = pulls(0, box_now)
     forces(0, value_ref)
     box_next = 2.0 * box_now - box_before + STEP_SCALE * pull / mass
@@ -573,6 +585,7 @@
 
     repeat(1, BOX, sample_peer)
     sample_block(1, j)
+    first_forces(next_ref)
     pull = pulls(1, box_next)
     box_after = 2.0 * box_next - box_now + STEP_SCALE * pull / mass
     for m in range(8):
@@ -581,9 +594,7 @@
     returned[i] = ways[lax.div(i, 2)]
     forces(1, next_ref)
     reactions(1)
-    advance(j, next_ref, value_ref, force_ref, sum_ref, node_mass_ref, modes_ref, last_ref)
-    result = pltpu.make_async_copy(last_ref, out_ref, out_sem.at[0])
-    result.start()
+    advance(j, next_ref, value_ref, force_ref, sum_ref, node_mass_ref, modes_ref, out_ref)
 
     repeat(1, MER, lambda o: to_back(o).wait_recv())
     even = jnp.concatenate([returned[2 * r, 0:1, :] for r in range(8)], axis=0)
@@ -594,8 +605,7 @@
     for r in range(8):
         out = dot(pieces, hot(iota((1024, 128), 0) == dest_ref[r : r + 1, :]))
         box_last[r : r + 1, :] = out[0:1] + (out[1:2] + out[2:3])
-    box_result = pltpu.make_async_copy(box_last, box_out_ref, out_sem.at[1])
-    box_result.start()
+    box_out_ref[...] = box_last[...]
 
     def sent(o):
         to_share(o).wait_send()
@@ -613,29 +623,17 @@
     for step in range(2):
         for copy in to_edges(step):
             copy.wait_send()
-    result.wait()
-    box_result.wait()
-
-
-def hand_over_kernel(final_ref, box_ref, out_ref, box_out_ref, final, box, sem):
-    half = NODES * COLS // 2
-    parts = [
-        (final_ref.at[k * half : (k + 1) * half], final.at[k * half : (k + 1) * half],
-         out_ref.at[k * half : (k + 1) * half])
-        for k in range(2)
-    ] + [(box_ref, box, box_out_ref)]
+
+
+def hand_over_kernel(final_ref, box_ref, out_ref, box_out_ref, sem):
     copies = [
-        (pltpu.make_async_copy(source, middle, sem.at[0, k]),
-         pltpu.make_async_copy(middle, target, sem.at[1, k]))
-        for k, (source, middle, target) in enumerate(parts)
+        pltpu.make_async_copy(final_ref, out_ref, sem.at[0]),
+        pltpu.make_async_copy(box_ref, box_out_ref, sem.at[1]),
     ]
-    for first, second in copies:
-        first.start()
-    for first, second in copies:
-        first.wait()
-        second.start()
-    for first, second in copies:
-        second.wait()
+    for copy in copies:
+        copy.start()
+    for copy in copies:
+        copy.wait()
 
 
 def per_device(
@@ -701,20 +699,20 @@
     final, box_out = pl.pallas_call(
         whole_kernel,
         out_shape=[jax.ShapeDtypeStruct((flat, ELEMS), F32), jax.ShapeDtypeStruct((8, 128), F32)],
-        in_specs=[any_space] * INPUTS,
-        out_specs=[any_space] * 2,
+        in_specs=[pl.BlockSpec(memory_space=pltpu.HBM)] * INPUTS,
+        out_specs=[pl.BlockSpec(memory_space=pltpu.VMEM)] * 2,
         scratch_shapes=scratch,
         compiler_params=pltpu.CompilerParams(
-            vmem_limit_bytes=56 << 20, collective_id=0, has_side_effects=True),
+            vmem_limit_bytes=44 << 20, collective_id=0, has_side_effects=True),
         name="coupled_steps",
-    )(*args)
+    )(*[pltpu.with_memory_space_constraint(x, pltpu.HBM) for x in args])
     final, box_out = pl.pallas_call(
         hand_over_kernel,
         out_shape=[jax.ShapeDtypeStruct((flat, ELEMS), F32), jax.ShapeDtypeStruct((8, 128), F32)],
-        in_specs=[any_space] * 2,
+        in_specs=[pl.BlockSpec(memory_space=pltpu.VMEM)] * 2,
         out_specs=[any_space] * 2,
-        scratch_shapes=[vmem((flat, ELEMS), F32), vmem((8, 128), F32), dma((2, 3))],
-        compiler_params=pltpu.CompilerParams(vmem_limit_bytes=60 << 20),
+        scratch_shapes=[dma((2,))],
+        compiler_params=pltpu.CompilerParams(vmem_limit_bytes=4 << 20),
         name="hand_over",
     )(final, box_out)
     return final.reshape(NODES, COLS, ELEMS), box_out.reshape(1024)

time: 51.8 us -> 48.1 us (0.929)
  Pallas kernels: 51 us -> 47.3 us
    pallas_call x1, Pallas kernels: 49.1 us -> 46.4 us  [per_device(): pl.pallas_call(whole_kernel, out_shape=[jax.ShapeDtypeStruct((flat, ELEMS...]
    pallas_call x1, Pallas kernels: 1.94 us -> 0.91 us  [per_device(): pl.pallas_call(hand_over_kernel, out_shape=[jax.ShapeDtypeStruct((flat, E...]
where the time goes in v5:
time: 48.1 us; the launch traced here: 48 us
  Pallas kernels  47.3 us (98%)
  between operations  0.65 us (1%)
    pallas_call x1, Pallas kernels, per_device(): pl.pallas_call(whole_kernel, out_shape=[jax.ShapeDtypeStruct((flat, ELEMS...  46.4 us

profile of v5, /device:TPU:1, one launch (start us, length us, event | category | flops | bytes accessed | tf_op | source)
XLA Modules:
  0.0 48.0 jit_solution(15586340208068830787)
XLA Ops:
  0.6 46.4 %coupled_steps.1 = (f32[1600,128]{1,0:T(8,128)S(1)}, f32[8,128]{1,0:T(8,128)S(1)}) custom-call(f32[8,128]{1,0:T(8,128)} %bitcast.20, s32[8,128]{1,0:T(8,128)} %bitcast.21, f32[8,128]{1,0:T(8,128)} %bitcast.22, f32[8,128]{1,0:T(8,128)} %bitcast.23, f32[8,128]{1,0:T(8,128)} %bitcast.24, f32[8,128]{1,0:T(8,128)} %bitcast.25, f32[8,128]{1,0:T(8,128)} %bitcast.26, ...), custom_call_target="tpu_custom_call" | custom-call | tf_op jit(solution)/shard_map/coupled_steps/pallas_call | solution.py:699
  47.1 0.9 %hand_over.1 = (f32[1600,128]{1,0:T(8,128)}, f32[8,128]{1,0:T(8,128)}) custom-call(f32[1600,128]{1,0:T(8,128)S(1)} %get-tuple-element.6.final_ref, f32[8,128]{1,0:T(8,128)S(1)} %get-tuple-element.7.box_ref), custom_call_target="tpu_custom_call" | custom-call | tf_op jit(solution)/shard_map/hand_over/pallas_call | solution.py:709

commit v6 on v5

--- a/solution.py
+++ b/solution.py
@@ -590,9 +590,9 @@
     box_after = 2.0 * box_next - box_now + STEP_SCALE * pull / mass
     for m in range(8):
         ways[m] = jnp.broadcast_to(box_after[m : m + 1, :], (8, 128))
+    forces(1, next_ref)
     repeat(1, MER, lambda o: to_back(o).start())
     returned[i] = ways[lax.div(i, 2)]
-    forces(1, next_ref)
     reactions(1)
     advance(j, next_ref, value_ref, force_ref, sum_ref, node_mass_ref, modes_ref, out_ref)
 

time: 48.1 us -> 48.1 us (level)
  no operation moved by 1% of the time
where the time goes in v6:
time: 48.1 us; the launch traced here: 48 us
  Pallas kernels  47.3 us (98%)
  between operations  0.65 us (1%)
    pallas_call x1, Pallas kernels, per_device(): pl.pallas_call(whole_kernel, out_shape=[jax.ShapeDtypeStruct((flat, ELEMS...  46.4 us

profile of v6, /device:TPU:1, one launch (start us, length us, event | category | flops | bytes accessed | tf_op | source)
XLA Modules:
  0.0 48.0 jit_solution(1873752771586585547)
XLA Ops:
  0.6 46.4 %coupled_steps.1 = (f32[1600,128]{1,0:T(8,128)S(1)}, f32[8,128]{1,0:T(8,128)S(1)}) custom-call(f32[8,128]{1,0:T(8,128)} %bitcast.20, s32[8,128]{1,0:T(8,128)} %bitcast.21, f32[8,128]{1,0:T(8,128)} %bitcast.22, f32[8,128]{1,0:T(8,128)} %bitcast.23, f32[8,128]{1,0:T(8,128)} %bitcast.24, f32[8,128]{1,0:T(8,128)} %bitcast.25, f32[8,128]{1,0:T(8,128)} %bitcast.26, ...), custom_call_target="tpu_custom_call" | custom-call | tf_op jit(solution)/shard_map/coupled_steps/pallas_call | solution.py:699
  47.1 0.9 %hand_over.1 = (f32[1600,128]{1,0:T(8,128)}, f32[8,128]{1,0:T(8,128)}) custom-call(f32[1600,128]{1,0:T(8,128)S(1)} %get-tuple-element.6.final_ref, f32[8,128]{1,0:T(8,128)S(1)} %get-tuple-element.7.box_ref), custom_call_target="tpu_custom_call" | custom-call | tf_op jit(solution)/shard_map/hand_over/pallas_call | solution.py:709
